TPU v7x, 128 devices: a whole 4x4x4 slice. The times are simulated.
128 devices in a mesh: front: 16 (over y, x_lo, core), blk: 8 (over x_hi, z).
Axes of the slice: x: 4 (x_hi: 2, x_lo: 2; x = x_hi * 2 + x_lo), y: 4, z: 4, core: 2. Of those that a mesh axis runs over, the one named last changes fastest.
Arguments:
- factor_rows: float32 [16, 4096, 1024], P('front', 'blk'), may hold values from -0.375 to 0.375
- front_sizes: int32 [16], P('front'), may hold values from 4 to 8
- tile_counts: int32 [16], replicated, may hold values from 29 to 32
- parent_tiles: int32 [16, 32, 32], replicated, may hold values from 0 to 1023, as said below
- parent_entries: float32 [1024, 128, 128], P(('front', 'blk')), may hold values from -6 to 6
Outputs:
- parent_update: float32 [1024, 128, 128], P(('front', 'blk'))
Inputs may be any that keep to these rules, and one draw needn't show every extreme that they name: `parent_tiles`: parent tile p is owned by the device of linear index p // 8 over front and blk (front slowest). Among the tiles of the rows of one device (its 4 index blocks of rows, all 32 columns), no owner is named more than 2 times; one owner is named exactly 2 times by every device, by tiles of the device's first row block in columns below 2.
All inputs are finite; a program needn't handle non-finite values.
Results may differ from a plain program's by a relative error of at most 0.0003.
Values sent between devices are 32-bit elements; how exact they have to be, the bound alone decides.
A program may use at most 128 MiB of HBM per device.

v0:
```python
import jax
import jax.numpy as jnp
from jax import lax
from jax.sharding import PartitionSpec as P

K = 1024
TR = 128
PT_DEV = 8


def per_device(factor_rows, front_sizes, tile_counts, parent_tiles, parent_entries):
    group_size = lax.axis_size("blk")
    front_count = lax.axis_size("front")
    own_block = lax.axis_index("blk")
    own_front = lax.axis_index("front")
    device_count = front_count * group_size
    own_device = own_front * group_size + own_block
    column_ids = jnp.arange(K, dtype=jnp.int32)
    own_rows = jnp.where((column_ids < front_sizes[0] * TR)[None, :], factor_rows[0], 0.0)
    block_rows = own_rows.shape[0]
    row_blocks = block_rows // TR
    extend_blocks = row_blocks * group_size
    capacity = max(2, 3 * row_blocks * row_blocks // (2 * front_count))
    tile_total = row_blocks * extend_blocks
    slot_count = device_count * capacity
    schur_rows = lax.dot_general(
        own_rows,
        lax.all_gather(own_rows, "blk", axis=0, tiled=True),
        (((1,), (1,)), ((), ())),
        precision=lax.Precision.HIGHEST,
        preferred_element_type=jnp.float32,
    )
    tile_ids = jnp.arange(tile_total, dtype=jnp.int32)
    all_targets = parent_tiles.reshape(device_count, tile_total)
    source_block = jnp.arange(device_count, dtype=jnp.int32) % group_size
    row_block = source_block[:, None] * row_blocks + (tile_ids // extend_blocks)[None, :]
    col_block = (tile_ids % extend_blocks)[None, :]
    group_counts = jnp.repeat(tile_counts, group_size)[:, None]
    live_all = (row_block < group_counts) & (col_block < group_counts)
    owner_all = all_targets // PT_DEV
    local_all = all_targets % PT_DEV
    live_own = lax.dynamic_index_in_dim(live_all, own_device, 0, keepdims=False)
    owner_own = lax.dynamic_index_in_dim(owner_all, own_device, 0, keepdims=False)
    same_owner = (
        (owner_own[:, None] == owner_own[None, :])
        & live_own[None, :]
        & (tile_ids[None, :] < tile_ids[:, None])
    )
    rank_own = jnp.sum(same_owner.astype(jnp.int32), axis=1)
    slot_index = jnp.where(live_own, owner_own * capacity + rank_own, slot_count)
    source_tile = (
        jnp.full((slot_count,), tile_total, jnp.int32).at[slot_index].set(tile_ids, mode="drop")
    )
    filled = source_tile < tile_total
    clamped = jnp.minimum(source_tile, tile_total - 1)
    schur_tiles = schur_rows.reshape(row_blocks, TR, extend_blocks, TR)
    picked = schur_tiles[clamped // extend_blocks, :, clamped % extend_blocks, :]
    outgoing = jnp.where(filled[:, None, None], picked, 0.0).reshape(slot_count, TR * TR)
    incoming = lax.all_to_all(outgoing, ("front", "blk"), split_axis=0, concat_axis=0, tiled=True)
    mine_all = live_all & (owner_all == own_device)
    rank_all = jnp.cumsum(mine_all.astype(jnp.int32), axis=1) - 1
    by_slot = (
        rank_all[:, :, None] == jnp.arange(capacity, dtype=jnp.int32)[None, None, :]
    ) & mine_all[:, :, None]
    by_local = local_all[:, :, None] == jnp.arange(PT_DEV, dtype=jnp.int32)[None, None, :]
    assemble = jnp.einsum(
        "stc,stp->psc", by_slot.astype(jnp.float32), by_local.astype(jnp.float32)
    ).reshape(PT_DEV, slot_count)
    summed = jnp.dot(
        assemble, incoming, precision=lax.Precision.HIGHEST, preferred_element_type=jnp.float32
    )
    return parent_entries - summed.reshape(PT_DEV, TR, TR)


def solution(mesh):
    in_specs = (P("front", "blk", None), P("front"), P(), P(), P(("front", "blk"), None, None))
    out_specs = P(("front", "blk"), None, None)
    return jax.shard_map(
        per_device, mesh=mesh, in_specs=in_specs, out_specs=out_specs, check_vma=False
    )
```

profile of v0, /device:TPU:105, one launch (start us, length us, event | category | flops | bytes accessed | tf_op | source)
XLA Modules:
  0.0 578.1 jit_solution(432279639501534917)
XLA Ops:
  6.5 0.0 all-gather.2.cloned.1.call-start
  7.2 3.2 bitcast_select_fusion
  10.4 0.0 all-gather.2.cloned.1.call-update
  10.5 1.1 reshape.344
  11.5 0.1 copy.24
  11.6 0.7 broadcast_in_dim.59
  12.4 0.1 lt.110
  12.5 0.1 fusion.16
  12.6 0.2 dynamic-slice_reduce_fusion
  12.8 0.2 multiply_reduce_fusion
  13.0 0.2 convert_reduce_fusion
  13.2 1.0 scatter_custom_fusion
  14.2 0.2 broadcast_in_dim.61
  14.4 1.8 broadcast_select_fusion.1
  16.1 175.2 %all-gather.2.cloned.1.call-done = f32[4096,1024]{1,0:T(8,128)} async-done(((f32[512,1024]{1,0:T(8,128)}), f32[4096,1024]{1,0:T(8,128)}) %all-gather.2.cloned.1.call-update) | async-done | bytes 16777232 | tf_op jit(solution)/shard_map/all_gather | solution.py:28
  191.3 31.8 %fusion.17 = f32[4,128,32,128]{3,1,2,0:T(8,128)} fusion(f32[4,128,1024,1]{2,1,3,0:T(8,128)S(1)} %bitcast.42, f32[32,128,1024,1]{2,1,0,3:T(8,128)} %bitcast.44), kind=kOutput, calls=%fused_computation.57 | convolution fusion | flops 25769803776 | bytes 27262976 | tf_op jit(solution)/shard_map/dot_general | solution.py:26
  223.1 16.2 %gather_fusion = f32[256,128,128]{2,1,0:T(8,128)} fusion(f32[4,128,32,128]{3,1,2,0:T(8,128)} %fusion.17, s32[256]{0:T(256)S(1)} %fusion.11), kind=kCustom, calls=%fused_computation | custom fusion | bytes 33556480 | tf_op jit(solution)/shard_map/gather | solution.py:57
  239.3 19.8 %gather.6 = f32[128,2,16384]{2,1,0:T(2,128)} reshape(f32[256,128,128]{2,1,0:T(8,128)} %gather_fusion) | data formatting | bytes 33554432 | tf_op jit(solution)/shard_map/gather | solution.py:57
  259.0 12.2 %broadcast_select_fusion = f32[128,2,16384]{2,1,0:T(2,128)} fusion(f32[128,2,16384]{2,1,0:T(2,128)} %gather.6, pred[128,2]{1,0:T(8,128)(4,1)S(1)} %broadcast_in_dim.61), kind=kLoop, calls=%fused_computation.2 | loop fusion | flops 4194304 | bytes 33554688 | tf_op jit(solution)/shard_map/jit(_where)/select_n | solution.py:58
  271.2 10.0 %all-to-all-start = ((f32[128,2,16384]{2,1,0:T(2,128)}), f32[128,2,16384]{2,1,0:T(2,128)}, u32[]{:S(2)}, u32[]{:S(2)}) async-start(f32[128,2,16384]{2,1,0:T(2,128)} %broadcast_select_fusion), calls=%async_computation | async-start | bytes 33554432 | tf_op jit(solution)/shard_map/all_to_all | solution.py:59
  281.3 0.1 copy.27
  281.4 0.1 copy.30
  281.5 0.2 reduce_window_sum.11
  281.7 0.1 copy.29
  281.8 0.3 fusion
  282.1 233.7 %all-to-all-done = f32[128,2,16384]{2,1,0:T(2,128)} async-done(((f32[128,2,16384]{2,1,0:T(2,128)}), f32[128,2,16384]{2,1,0:T(2,128)}, u32[]{:S(2)}, u32[]{:S(2)}) %all-to-all-start) | async-done | bytes 16777248 | tf_op jit(solution)/shard_map/all_to_all | solution.py:59
  515.8 20.5 %all_to_all.7 = f32[256,16384]{1,0:T(8,128)} reshape(f32[128,2,16384]{2,1,0:T(2,128)} %all-to-all-done) | data formatting | bytes 33554432 | tf_op jit(solution)/shard_map/all_to_all | solution.py:59
  536.3 0.0 copy-start
  536.3 17.5 %copy.31 = f32[256,16384]{0,1:T(8,128)} copy(f32[256,16384]{1,0:T(8,128)} %all_to_all.7) | data formatting | bytes 33554432 | tf_op jit(solution)/shard_map/all_to_all | solution.py:59
  553.8 0.0 copy-done
  553.8 16.5 %convolution_subtract_fusion = f32[8,128,128]{2,0,1:T(8,128)S(1)} fusion(f32[8,256,1]{0,1,2:T(8,128)S(1)} %bitcast.43, f32[128,128,256]{2,1,0:T(8,128)} %bitcast.41, f32[8,128,128]{2,1,0:T(8,128)S(1)} %copy-done), kind=kOutput, calls=%fused_computation.4 | convolution fusion | flops 402784256 | bytes 17833984 | tf_op jit(solution)/shard_map/dot_general | solution.py:69
  570.3 0.9 copy.34
  (9 shorter events, 0.1 us)
Async XLA Ops:
  6.5 184.8 %all-gather.2.cloned.1.call-start = ((), (), s32[]{:S(2)}) async-start(), calls=%async_computation.1 | async-start | bytes 18874368 | tf_op jit(solution)/shard_map/all_gather | solution.py:28
  271.2 244.5 %all-to-all-start = ((f32[128,2,16384]{2,1,0:T(2,128)}), f32[128,2,16384]{2,1,0:T(2,128)}, u32[]{:S(2)}, u32[]{:S(2)}) async-start(f32[128,2,16384]{2,1,0:T(2,128)} %broadcast_select_fusion), calls=%async_computation | async-start | bytes 33554432 | tf_op jit(solution)/shard_map/all_to_all | solution.py:59
  536.3 17.5 %copy-start = (f32[8,128,128]{2,1,0:T(8,128)S(1)}, f32[8,128,128]{2,1,0:T(8,128)}, u32[]{:S(2)}) copy-start(f32[8,128,128]{2,1,0:T(8,128)} %param.9) | copy-start | bytes 1572868
Sparse Core Ops, SparseCore 0:
  10.6 180.6 all-gather.1
where the time goes:
time: 579 us; the launch traced here: 578 us
  waiting for transfers between devices  409 us (71%)
  local copies, waits for them, and re-layouts  78.5 us (14%)
  matrix products  48.6 us (8%)
  other arithmetic  17.9 us (3%)
  between operations  14.2 us (2%)
  starting transfers between devices  10 us (2%)
    all_to_all x1, waiting for transfers between devices, per_device(): lax.all_to_all(outgoing, ('front', 'blk'), split_axis=0, concat_axis=0, t...  234 us
    all_gather x1, waiting for transfers between devices, per_device(): lax.all_gather(own_rows, 'blk', axis=0, tiled=True)  175 us
    all_to_all x2, local copies, waits for them, and re-layouts, per_device(): lax.all_to_all(outgoing, ('front', 'blk'), split_axis=0, concat_axis=0, t...  38.1 us
    gather x2, local copies, waits for them, and re-layouts, per_device(): schur_tiles[clamped // extend_blocks, :, clamped % extend_blocks, :]  35.9 us
    dot_general x1, matrix products, per_device(): lax.dot_general(own_rows, lax.all_gather(own_rows, 'blk', axis=0, tiled=T...  31.8 us
    dot_general x1, matrix products, per_device(): jnp.dot(assemble, incoming, precision=lax.Precision.HIGHEST, preferred_el...  16.5 us
    select_n x1, other arithmetic, per_device(): jnp.where(filled[:, None, None], picked, 0.0).reshape(slot_count, TR * TR)  12.2 us
  transfers between devices with their start and end apart: 2, of which 2 were waited for; matrix products, arithmetic and copies ran while one was open for 1% of the time, Pallas kernels for 0%

commit v1 on v0

v1 whole, which is shorter than its diff:
```python
import functools

import jax
import jax.numpy as jnp
from jax import lax
from jax.experimental import pallas as pl
from jax.experimental.pallas import tpu as pltpu
from jax.sharding import PartitionSpec as P

TR = 128
KH = 512
CB = 4
EB = 32
UNROLL = 4

MESH = pl.DeviceIdType.MESH
F32 = jnp.float32
BF16 = jnp.bfloat16


def position():
    front, blk = lax.axis_index("front"), lax.axis_index("blk")
    return dict(
        front=front,
        blk=blk,
        y=front // 4,
        xl=(front // 2) % 2,
        core=front % 2,
        xh=blk // 4,
        z=blk % 4,
    )


def device(p, **moves):
    q = {**p, **moves}
    return {"front": q["y"] * 4 + q["xl"] * 2 + q["core"], "blk": q["xh"] * 4 + q["z"]}


def slot(xs, dz, c):
    return (xs * 4 + dz) * CB + c


def gather_kernel(
    x, parents, fs, counts, hl, lists, tile_counts,
    mine, other, split, fs_other,
    x_send, z_send, recv, core_send, core_recv, local, out_sem, fs_sem,
):
    p = position()
    z, xh = p["z"], p["xh"]
    up, down = device(p, z=(z + 1) % 4), device(p, z=(z + 3) % 4)
    across = device(p, xh=1 - xh)
    twin = device(p, core=1 - p["core"])

    barrier = pltpu.get_barrier_semaphore()
    for other_dev in (up, down, across, twin):
        pl.semaphore_signal(barrier, inc=1, device_id=other_dev, device_id_type=MESH)
    pl.semaphore_wait(barrier, 4)

    sent = []
    ready = []

    def send(src, dst, ssem, rsem, to):
        copy = pltpu.make_async_remote_copy(
            src_ref=src, dst_ref=dst, send_sem=ssem, recv_sem=rsem, device_id=to, device_id_type=MESH
        )
        copy.start()
        sent.append(copy)

    n_z = [0]

    def send_z(src, xs, dz, c, to):
        s = slot(xs, dz, c)
        send(src, mine.at[s], z_send.at[n_z[0]], recv.at[s], to)
        n_z[0] += 1

    def arrived(s):
        pltpu.make_async_remote_copy(
            src_ref=mine.at[s], dst_ref=mine.at[s], send_sem=z_send.at[0], recv_sem=recv.at[s],
            device_id=up, device_id_type=MESH,
        ).wait_recv()

    def to_twin(s):
        send(mine.at[s], other.at[s], core_send.at[s], core_recv.at[s], twin)

    def from_twin(s):
        pltpu.make_async_remote_copy(
            src_ref=mine.at[s], dst_ref=other.at[s], send_sem=core_send.at[s], recv_sem=core_recv.at[s],
            device_id=twin, device_id_type=MESH,
        ).wait_recv()

    own_cols = pl.ds(pl.multiple_of(xh * KH, KH), KH)
    across_cols = pl.ds(pl.multiple_of((1 - xh) * KH, KH), KH)

    def rows(c):
        return pl.ds(c * TR, TR)

    send(fs, fs_other, fs_sem.at[0], fs_sem.at[1], twin)
    fs_copy = sent[-1]
    loads = []
    for c in (0, 2, 1, 3):
        s = slot(1, 0, c)
        send(x.at[rows(c), across_cols], mine.at[s], x_send.at[c], recv.at[s], across)
    for c, d in ((0, 2), (1, 3), (2, 0), (3, 1)):
        send_z(x.at[rows(c), own_cols], 0, 3, c, up)
        send_z(x.at[rows(d), own_cols], 0, 1, d, down)
        load = pltpu.make_async_copy(x.at[rows(c), own_cols], mine.at[slot(0, 0, c)], local.at[c])
        load.start()
        loads.append(load)

    col = lax.broadcasted_iota(jnp.int32, (EB, EB), 1)
    row = lax.broadcasted_iota(jnp.int32, (EB, EB), 0)
    lower = (row >= col).astype(F32)
    for g in range(2):
        f = (p["front"] // 2) * 2 + (p["core"] if g == 0 else 1 - p["core"])
        target = parents[f]
        live = counts[f][0:1, 0:EB]
        dest = target >> 3
        dest_front, dest_blk = dest >> 3, dest & 7
        hit = ((dest_blk & 3) == z) & ((dest_front & 1) == p["core"])
        hit = hit & (row < live) & (col < live)
        rx = ((dest_blk >> 2) * 2 + ((dest_front >> 1) & 1) - (p["xh"] * 2 + p["xl"])) & 3
        ry = ((dest_front >> 2) - p["y"]) & 3
        place = target & 7
        first = place < 4
        at = jnp.where(first, ry * 4 + rx, 16 + rx * 4 + ry) * 4 + (place & 3)
        code = (col << 13) + (row << 8) + at
        rank = jnp.dot(lower, hit.astype(F32), preferred_element_type=F32).astype(jnp.int32)
        tile_counts[g : g + 1, 0:EB] = rank[EB - 1 : EB, :]
        rank = jnp.where(hit, rank, 0)
        for k in range(EB):
            lists[g, k : k + 1, 0:EB] = jnp.sum(jnp.where(rank == k + 1, code, 0), axis=0, keepdims=True)

    def convert(g, s):
        src = mine if g == 0 else other
        size = (fs if g == 0 else fs_other)[0:1, :]
        block = lax.broadcasted_iota(jnp.int32, (1, KH), 1) // TR + xh * (KH // TR)
        keep = block < size

        def step(i, _):
            at = pl.multiple_of(i * 16, 16)
            v = jnp.where(keep, src[s, pl.ds(at, 16), :], 0.0)
            hi = v.astype(BF16)
            split[g, s, pl.ds(at, 16), :] = hi
            split[g, s, pl.ds(TR + at, 16), :] = (v - hi.astype(F32)).astype(BF16)
            return 0

        lax.fori_loop(0, TR // 16, step, 0)
        ready.append((g, s))

    outs = []

    def put():
        g, s = ready.pop(0)
        xs, dz, c = s // 16, (s // 4) % 4, s % 4
        blk = (xh if xs == 0 else 1 - xh) * 4 + (z + dz) % 4
        copy = pltpu.make_async_copy(split.at[g, s], hl.at[g, blk * CB + c], out_sem.at[g * 32 + s])
        copy.start()
        outs.append(copy)

    twin_queue = []

    def take(s):
        to_twin(s)
        convert(0, s)
        twin_queue.append(s)
        if len(ready) > 1:
            put()
        if len(twin_queue) > 4:
            drain()

    def drain():
        t = twin_queue.pop(0)
        from_twin(t)
        convert(1, t)
        if len(ready) > 1:
            put()

    fs_copy.wait_recv()
    for c, load in zip((0, 1, 2, 3), loads):
        load.wait()
        take(slot(0, 0, c))
    for i in range(4):
        c, d = (0, 1, 2, 3)[i], (2, 3, 0, 1)[i]
        arrived(slot(0, 3, c))
        if c < 2:
            send_z(mine.at[slot(0, 3, c)], 0, 2, c, up)
        take(slot(0, 3, c))
        arrived(slot(0, 1, d))
        if d >= 2:
            send_z(mine.at[slot(0, 1, d)], 0, 2, d, down)
        take(slot(0, 1, d))
        e = (0, 2, 1, 3)[i]
        s = slot(1, 0, e)
        arrived(s)
        send_z(mine.at[s], 1, 3, e, up)
        send_z(mine.at[s], 1, 1, e, down)
        take(s)
    for e in (0, 2, 1, 3):
        arrived(slot(0, 2, e))
        take(slot(0, 2, e))
    for e in (0, 2, 1, 3):
        s = slot(1, 3, e)
        arrived(s)
        if e < 2:
            send_z(mine.at[s], 1, 2, e, up)
        take(s)
        s = slot(1, 1, e)
        arrived(s)
        if e >= 2:
            send_z(mine.at[s], 1, 2, e, down)
        take(s)
    for e in (0, 2, 1, 3):
        arrived(slot(1, 2, e))
        take(slot(1, 2, e))
    while twin_queue:
        drain()
    while ready:
        put()
    for copy in sent:
        copy.wait_send()
    for copy in outs:
        copy.wait()


def tiles_kernel(lists, counts, hl, out, held, acc, flat, load_sem, out_sem):
    loads = []
    for g in range(2):
        for q in range(4):
            part = pl.ds(q * 8, 8)
            load = pltpu.make_async_copy(hl.at[g, part], held.at[g, part], load_sem.at[g * 4 + q])
            load.start()
            loads.append(load)

    def clear(i, _):
        acc[i] = jnp.zeros((TR, TR), F32)
        return 0

    lax.fori_loop(0, 129, clear, 0)

    totals = []
    for g in range(2):
        def column(b, n):
            def entry(k, n):
                flat[g, n] = lists[g, k, b]
                return n + 1

            return lax.fori_loop(0, counts[g, b], entry, n)

        n = lax.fori_loop(0, EB, column, 0)
        for u in range(UNROLL - 1):
            flat[g, n + u] = 128
        totals.append(n)

    for g in range(2):
        for q in range(4):
            loads[g * 4 + q].wait()

        def several(i, _):
            for u in range(UNROLL):
                code = flat[g, i * UNROLL + u]
                b, a, at = code >> 13, (code >> 8) & 31, code & 255
                d = lax.dot_general(
                    held[g, a], held[g, b], (((1,), (1,)), ((), ())), preferred_element_type=F32
                )
                acc[at] += d[:TR, :TR] + (d[:TR, TR:] + d[TR:, :TR])
            return 0

        lax.fori_loop(0, (totals[g] + UNROLL - 1) // UNROLL, several, 0)

    copy = pltpu.make_async_copy(acc.at[pl.ds(0, 128)], out, out_sem)
    copy.start()
    copy.wait()


def scatter_kernel(
    part, out, data, opp, near, fwd, mid, mid_opp, mid_near, mid_fwd, res,
    send_sem, recv_sem, load_sem,
):
    p = position()
    x = p["xh"] * 2 + p["xl"]

    def along_x(d):
        n = (x + d) % 4
        return device(p, xh=n // 2, xl=n % 2)

    def along_y(d):
        return device(p, y=(p["y"] + d) % 4)

    barrier = pltpu.get_barrier_semaphore()
    for to in (along_x(1), along_x(3), along_y(1), along_y(3)):
        pl.semaphore_signal(barrier, inc=1, device_id=to, device_id_type=MESH)
    pl.semaphore_wait(barrier, 4)

    sent = []
    count = [0]

    def send(src, dst, to):
        k = count[0]
        count[0] += 1
        copy = pltpu.make_async_remote_copy(
            src_ref=src, dst_ref=dst, send_sem=send_sem.at[k], recv_sem=recv_sem.at[k],
            device_id=to, device_id_type=MESH,
        )
        copy.start()
        sent.append(copy)
        return copy

    def begin(src, n, h, to, opp, near):
        half = n // 2
        o_up = send(src(2, 0, half), opp.at[h, 0], to(1))
        o_down = send(src(2, half, half), opp.at[h, 1], to(3))
        n_up = send(src(1, half, half), near.at[h, 0, pl.ds(half, half)], to(1))
        n_down = send(src(3, 0, half), near.at[h, 1, pl.ds(0, half)], to(3))
        return o_up, o_down, n_up, n_down

    def relay(copies, val, n, h, to, opp, near, fwd):
        half = n // 2
        copies[0].wait_recv()
        fwd[h, 0] = val(1, 0, half) + opp[h, 0]
        f_up = send(fwd.at[h, 0], near.at[h, 0, pl.ds(0, half)], to(1))
        copies[1].wait_recv()
        fwd[h, 1] = val(3, half, half) + opp[h, 1]
        f_down = send(fwd.at[h, 1], near.at[h, 1, pl.ds(half, half)], to(3))
        return copies[2], copies[3], f_up, f_down

    ways = ((along_y, along_x), (along_x, along_y))
    firsts = []
    for h in range(2):
        firsts.append(
            begin(lambda r, lo, size: part.at[pl.ds(h * 64 + r * 16 + lo, size)], 16, h, ways[h][0], opp, near)
        )
    loads = []
    for h in range(2):
        for r in (1, 3, 0):
            sl = pl.ds(h * 64 + r * 16, 16)
            load = pltpu.make_async_copy(part.at[sl], data.at[sl], load_sem.at[h * 4 + r])
            load.start()
            loads.append(load)
    for load in loads:
        load.wait()

    seconds = []
    for h in range(2):
        firsts[h] = relay(
            firsts[h], lambda r, lo, size: data[pl.ds(h * 64 + r * 16 + lo, size)], 16, h, ways[h][0], opp, near, fwd
        )
    for h in range(2):
        for copy in firsts[h]:
            copy.wait_recv()
        mid[h] = data[pl.ds(h * 64, 16)] + (near[h, 0] + near[h, 1])
        seconds.append(
            begin(lambda r, lo, size: mid.at[h, pl.ds(r * 4 + lo, size)], 4, h, ways[h][1], mid_opp, mid_near)
        )
    for h in range(2):
        seconds[h] = relay(
            seconds[h], lambda r, lo, size: mid[h, pl.ds(r * 4 + lo, size)], 4, h, ways[h][1], mid_opp, mid_near, mid_fwd
        )
    for h in range(2):
        for copy in seconds[h]:
            copy.wait_recv()
        out[pl.ds(h * 4, 4)] = mid[h, pl.ds(0, 4)] + (mid_near[h, 0] + mid_near[h, 1])
    for copy in sent:
        copy.wait_send()


def per_device(factor_rows, front_sizes, tile_counts, parent_tiles, parent_entries):
    any_space = pl.BlockSpec(memory_space=pl.ANY)
    vmem = pl.BlockSpec(memory_space=pltpu.VMEM)
    limit = 60 * 2**20
    fs = jnp.broadcast_to(front_sizes.reshape(1, 1), (8, KH))
    live = jnp.broadcast_to(tile_counts[:, None, None], (16, 8, 128))
    dma = pltpu.SemaphoreType.DMA
    hl, lists, counts = pl.pallas_call(
        gather_kernel,
        out_shape=(
            jax.ShapeDtypeStruct((2, EB, 2 * TR, KH), BF16),
            jax.ShapeDtypeStruct((2, EB, 128), jnp.int32),
            jax.ShapeDtypeStruct((8, 128), jnp.int32),
        ),
        in_specs=[any_space, vmem, vmem, vmem],
        out_specs=(any_space, vmem, vmem),
        scratch_shapes=[
            pltpu.VMEM((EB, TR, KH), F32),
            pltpu.VMEM((EB, TR, KH), F32),
            pltpu.VMEM((2, EB, 2 * TR, KH), BF16),
            pltpu.VMEM((8, KH), jnp.int32),
            dma((4,)),
            dma((24,)),
            dma((32,)),
            dma((32,)),
            dma((32,)),
            dma((4,)),
            dma((64,)),
            dma((2,)),
        ],
        compiler_params=pltpu.CompilerParams(collective_id=0, has_side_effects=True, vmem_limit_bytes=limit),
        name="gather",
    )(factor_rows[0], parent_tiles, fs, live)
    part = pl.pallas_call(
        tiles_kernel,
        out_shape=jax.ShapeDtypeStruct((128, TR, TR), F32),
        grid_spec=pltpu.PrefetchScalarGridSpec(
            num_scalar_prefetch=2,
            grid=(1,),
            in_specs=[any_space],
            out_specs=any_space,
            scratch_shapes=[
                pltpu.VMEM((2, EB, 2 * TR, KH), BF16),
                pltpu.VMEM((129, TR, TR), F32),
                pltpu.SMEM((2, 1024 + 128), jnp.int32),
                dma((8,)),
                dma,
            ],
        ),
        compiler_params=pltpu.CompilerParams(vmem_limit_bytes=limit),
        name="tiles",
    )(lists[:, :, :EB], counts[:2, :EB], hl)
    summed = pl.pallas_call(
        scatter_kernel,
        out_shape=jax.ShapeDtypeStruct((8, TR, TR), F32),
        in_specs=[any_space],
        out_specs=vmem,
        scratch_shapes=[
            pltpu.VMEM((128, TR, TR), F32),
            pltpu.VMEM((2, 2, 8, TR, TR), F32),
            pltpu.VMEM((2, 2, 16, TR, TR), F32),
            pltpu.VMEM((2, 2, 8, TR, TR), F32),
            pltpu.VMEM((2, 16, TR, TR), F32),
            pltpu.VMEM((2, 2, 2, TR, TR), F32),
            pltpu.VMEM((2, 2, 4, TR, TR), F32),
            pltpu.VMEM((2, 2, 2, TR, TR), F32),
            pltpu.VMEM((8, TR, TR), F32),
            dma((24,)),
            dma((24,)),
            dma((8,)),
        ],
        compiler_params=pltpu.CompilerParams(collective_id=1, has_side_effects=True, vmem_limit_bytes=limit),
        name="scatter",
    )(part)
    return parent_entries - summed


def solution(mesh):
    in_specs = (P("front", "blk", None), P("front"), P(), P(), P(("front", "blk"), None, None))
    out_specs = P(("front", "blk"), None, None)
    return jax.shard_map(
        per_device, mesh=mesh, in_specs=in_specs, out_specs=out_specs, check_vma=False
    )
```

time: 579 us -> 175 us (0.30)
  the two profiles are of different devices: /device:TPU:105 before, /device:TPU:1 now
where the time goes in v1:
time: 175 us
  Pallas kernels  169 us (97%)
  local copies, waits for them, and re-layouts  3.21 us (2%)
  other arithmetic  1.89 us (1%)
    pallas_call x1, Pallas kernels, per_device(): pl.pallas_call(gather_kernel, out_shape=(jax.ShapeDtypeStruct((2, EB, 2 *...  82.2 us
    pallas_call x1, Pallas kernels, per_device(): pl.pallas_call(scatter_kernel, out_shape=jax.ShapeDtypeStruct((8, TR, TR)...  45.5 us
    pallas_call x1, Pallas kernels, per_device(): pl.pallas_call(tiles_kernel, out_shape=jax.ShapeDtypeStruct((128, TR, TR)...  41 us

profile of v1, /device:TPU:1, one launch (start us, length us, event | category | flops | bytes accessed | tf_op | source)
XLA Modules:
  0.0 174.6 jit_solution(17974047932764950349)
XLA Ops:
  0.7 0.6 broadcast_in_dim.14.fs
  1.3 1.4 broadcast_in_dim.15.counts
  2.6 82.2 %gather.1 = (bf16[2,32,256,512]{3,2,1,0:T(8,128)(2,1)}, s32[2,32,128]{2,1,0:T(8,128)}, s32[8,128]{1,0:T(8,128)}) custom-call(f32[512,1024]{1,0:T(8,128)} %bitcast.4, s32[16,32,32]{2,1,0:T(8,128)} %parents.1, s32[8,512]{1,0:T(8,128)} %broadcast_in_dim.14.fs, s32[16,8,128]{2,1,0:T(8,128)} %broadcast_in_dim.15.counts), custom_call_target="tpu_custom_call" | custom-call | tf_op jit(solution)/shard_map/gather/pallas_call | solution.py:373
  84.8 1.2 slice.7.counts
  86.1 41.0 %tiles.1.part = f32[128,128,128]{2,1,0:T(8,128)} custom-call(s32[2,32,32]{2,1,0:T(8,128)} %bitcast.5, s32[2,32]{1,0:T(2,128)} %slice.7.counts, bf16[2,32,256,512]{3,2,1,0:T(8,128)(2,1)} %get-tuple-element.10.hl), custom_call_target="tpu_custom_call" | custom-call | tf_op jit(solution)/shard_map/tiles/pallas_call | solution.py:399
  127.1 0.0 copy-start
  127.1 45.5 %scatter.1 = f32[8,128,128]{2,1,0:T(8,128)} custom-call(f32[128,128,128]{2,1,0:T(8,128)} %tiles.1.part), custom_call_target="tpu_custom_call" | custom-call | tf_op jit(solution)/shard_map/scatter/pallas_call | solution.py:418
  172.7 0.0 copy-done
  172.7 1.9 %sub.3 = f32[8,128,128]{2,1,0:T(8,128)} subtract(f32[8,128,128]{2,1,0:T(8,128)S(1)} %copy-done, f32[8,128,128]{2,1,0:T(8,128)} %scatter.1) | non-fusion elementwise | flops 131072 | bytes 1572864 | tf_op jit(solution)/shard_map/sub | solution.py:440
Async XLA Ops:
  127.1 45.5 %copy-start = (f32[8,128,128]{2,1,0:T(8,128)S(1)}, f32[8,128,128]{2,1,0:T(8,128)}, u32[]{:S(2)}) copy-start(f32[8,128,128]{2,1,0:T(8,128)} %param.9) | copy-start | bytes 1572868

commit v2 on v1

--- a/solution.py
+++ b/solution.py
@@ -11,7 +11,7 @@
 KH = 512
 CB = 4
 EB = 32
-UNROLL = 4
+UNROLL = 16
 
 MESH = pl.DeviceIdType.MESH
 F32 = jnp.float32
@@ -41,9 +41,9 @@
 
 
 def gather_kernel(
-    x, parents, fs, counts, hl, lists, tile_counts,
-    mine, other, split, fs_other,
-    x_send, z_send, recv, core_send, core_recv, local, out_sem, fs_sem,
+    x, parents, sizes, counts, split, lists, tile_counts,
+    mine, other, fs, fs_other,
+    x_send, z_send, recv, core_send, core_recv, local, fs_sem,
 ):
     p = position()
     z, xh = p["z"], p["xh"]
@@ -51,13 +51,13 @@
     across = device(p, xh=1 - xh)
     twin = device(p, core=1 - p["core"])
 
+    fs[...] = jnp.full((8, KH), sizes[0], jnp.int32)
     barrier = pltpu.get_barrier_semaphore()
     for other_dev in (up, down, across, twin):
         pl.semaphore_signal(barrier, inc=1, device_id=other_dev, device_id_type=MESH)
     pl.semaphore_wait(barrier, 4)
 
     sent = []
-    ready = []
 
     def send(src, dst, ssem, rsem, to):
         copy = pltpu.make_async_remote_copy(
@@ -110,10 +110,14 @@
     col = lax.broadcasted_iota(jnp.int32, (EB, EB), 1)
     row = lax.broadcasted_iota(jnp.int32, (EB, EB), 0)
     lower = (row >= col).astype(F32)
+
+    def place_of(block):
+        return ((((block >> 4) ^ xh) << 4) + ((((block >> 2) - z) & 3) << 2)) + (block & 3)
+
     for g in range(2):
         f = (p["front"] // 2) * 2 + (p["core"] if g == 0 else 1 - p["core"])
         target = parents[f]
-        live = counts[f][0:1, 0:EB]
+        live = counts[f]
         dest = target >> 3
         dest_front, dest_blk = dest >> 3, dest & 7
         hit = ((dest_blk & 3) == z) & ((dest_front & 1) == p["core"])
@@ -123,7 +127,7 @@
         place = target & 7
         first = place < 4
         at = jnp.where(first, ry * 4 + rx, 16 + rx * 4 + ry) * 4 + (place & 3)
-        code = (col << 13) + (row << 8) + at
+        code = (place_of(col) << 13) + (place_of(row) << 8) + at
         rank = jnp.dot(lower, hit.astype(F32), preferred_element_type=F32).astype(jnp.int32)
         tile_counts[g : g + 1, 0:EB] = rank[EB - 1 : EB, :]
         rank = jnp.where(hit, rank, 0)
@@ -145,17 +149,6 @@
             return 0
 
         lax.fori_loop(0, TR // 16, step, 0)
-        ready.append((g, s))
-
-    outs = []
-
-    def put():
-        g, s = ready.pop(0)
-        xs, dz, c = s // 16, (s // 4) % 4, s % 4
-        blk = (xh if xs == 0 else 1 - xh) * 4 + (z + dz) % 4
-        copy = pltpu.make_async_copy(split.at[g, s], hl.at[g, blk * CB + c], out_sem.at[g * 32 + s])
-        copy.start()
-        outs.append(copy)
 
     twin_queue = []
 
@@ -163,8 +156,6 @@
         to_twin(s)
         convert(0, s)
         twin_queue.append(s)
-        if len(ready) > 1:
-            put()
         if len(twin_queue) > 4:
             drain()
 
@@ -172,8 +163,6 @@
         t = twin_queue.pop(0)
         from_twin(t)
         convert(1, t)
-        if len(ready) > 1:
-            put()
 
     fs_copy.wait_recv()
     for c, load in zip((0, 1, 2, 3), loads):
@@ -214,23 +203,11 @@
         take(slot(1, 2, e))
     while twin_queue:
         drain()
-    while ready:
-        put()
     for copy in sent:
         copy.wait_send()
-    for copy in outs:
-        copy.wait()
-
-
-def tiles_kernel(lists, counts, hl, out, held, acc, flat, load_sem, out_sem):
-    loads = []
-    for g in range(2):
-        for q in range(4):
-            part = pl.ds(q * 8, 8)
-            load = pltpu.make_async_copy(hl.at[g, part], held.at[g, part], load_sem.at[g * 4 + q])
-            load.start()
-            loads.append(load)
-
+
+
+def tiles_kernel(lists, counts, held, acc, flat):
     def clear(i, _):
         acc[i] = jnp.zeros((TR, TR), F32)
         return 0
@@ -252,9 +229,6 @@
         totals.append(n)
 
     for g in range(2):
-        for q in range(4):
-            loads[g * 4 + q].wait()
-
         def several(i, _):
             for u in range(UNROLL):
                 code = flat[g, i * UNROLL + u]
@@ -267,14 +241,10 @@
 
         lax.fori_loop(0, (totals[g] + UNROLL - 1) // UNROLL, several, 0)
 
-    copy = pltpu.make_async_copy(acc.at[pl.ds(0, 128)], out, out_sem)
-    copy.start()
-    copy.wait()
-
 
 def scatter_kernel(
-    part, out, data, opp, near, fwd, mid, mid_opp, mid_near, mid_fwd, res,
-    send_sem, recv_sem, load_sem,
+    part, out, opp, near, fwd, mid, mid_opp, mid_near, mid_fwd,
+    send_sem, recv_sem,
 ):
     p = position()
     x = p["xh"] * 2 + p["xl"]
@@ -329,25 +299,15 @@
         firsts.append(
             begin(lambda r, lo, size: part.at[pl.ds(h * 64 + r * 16 + lo, size)], 16, h, ways[h][0], opp, near)
         )
-    loads = []
-    for h in range(2):
-        for r in (1, 3, 0):
-            sl = pl.ds(h * 64 + r * 16, 16)
-            load = pltpu.make_async_copy(part.at[sl], data.at[sl], load_sem.at[h * 4 + r])
-            load.start()
-            loads.append(load)
-    for load in loads:
-        load.wait()
-
     seconds = []
     for h in range(2):
         firsts[h] = relay(
-            firsts[h], lambda r, lo, size: data[pl.ds(h * 64 + r * 16 + lo, size)], 16, h, ways[h][0], opp, near, fwd
+            firsts[h], lambda r, lo, size: part[pl.ds(h * 64 + r * 16 + lo, size)], 16, h, ways[h][0], opp, near, fwd
         )
     for h in range(2):
         for copy in firsts[h]:
             copy.wait_recv()
-        mid[h] = data[pl.ds(h * 64, 16)] + (near[h, 0] + near[h, 1])
+        mid[h] = part[pl.ds(h * 64, 16)] + (near[h, 0] + near[h, 1])
         seconds.append(
             begin(lambda r, lo, size: mid.at[h, pl.ds(r * 4 + lo, size)], 4, h, ways[h][1], mid_opp, mid_near)
         )
@@ -366,23 +326,21 @@
 def per_device(factor_rows, front_sizes, tile_counts, parent_tiles, parent_entries):
     any_space = pl.BlockSpec(memory_space=pl.ANY)
     vmem = pl.BlockSpec(memory_space=pltpu.VMEM)
-    limit = 60 * 2**20
-    fs = jnp.broadcast_to(front_sizes.reshape(1, 1), (8, KH))
-    live = jnp.broadcast_to(tile_counts[:, None, None], (16, 8, 128))
+    smem = pl.BlockSpec(memory_space=pltpu.SMEM)
     dma = pltpu.SemaphoreType.DMA
-    hl, lists, counts = pl.pallas_call(
+    split, lists, counts = pl.pallas_call(
         gather_kernel,
         out_shape=(
             jax.ShapeDtypeStruct((2, EB, 2 * TR, KH), BF16),
             jax.ShapeDtypeStruct((2, EB, 128), jnp.int32),
             jax.ShapeDtypeStruct((8, 128), jnp.int32),
         ),
-        in_specs=[any_space, vmem, vmem, vmem],
-        out_specs=(any_space, vmem, vmem),
+        in_specs=[any_space, vmem, smem, smem],
+        out_specs=(vmem, vmem, vmem),
         scratch_shapes=[
             pltpu.VMEM((EB, TR, KH), F32),
             pltpu.VMEM((EB, TR, KH), F32),
-            pltpu.VMEM((2, EB, 2 * TR, KH), BF16),
+            pltpu.VMEM((8, KH), jnp.int32),
             pltpu.VMEM((8, KH), jnp.int32),
             dma((4,)),
             dma((24,)),
@@ -390,38 +348,26 @@
             dma((32,)),
             dma((32,)),
             dma((4,)),
-            dma((64,)),
             dma((2,)),
         ],
-        compiler_params=pltpu.CompilerParams(collective_id=0, has_side_effects=True, vmem_limit_bytes=limit),
+        compiler_params=pltpu.CompilerParams(collective_id=0, has_side_effects=True, vmem_limit_bytes=20 * 2**20),
         name="gather",
-    )(factor_rows[0], parent_tiles, fs, live)
+    )(factor_rows[0], parent_tiles, front_sizes, tile_counts)
     part = pl.pallas_call(
         tiles_kernel,
-        out_shape=jax.ShapeDtypeStruct((128, TR, TR), F32),
-        grid_spec=pltpu.PrefetchScalarGridSpec(
-            num_scalar_prefetch=2,
-            grid=(1,),
-            in_specs=[any_space],
-            out_specs=any_space,
-            scratch_shapes=[
-                pltpu.VMEM((2, EB, 2 * TR, KH), BF16),
-                pltpu.VMEM((129, TR, TR), F32),
-                pltpu.SMEM((2, 1024 + 128), jnp.int32),
-                dma((8,)),
-                dma,
-            ],
-        ),
-        compiler_params=pltpu.CompilerParams(vmem_limit_bytes=limit),
+        out_shape=jax.ShapeDtypeStruct((129, TR, TR), F32),
+        in_specs=[smem, smem, vmem],
+        out_specs=vmem,
+        scratch_shapes=[pltpu.SMEM((2, 1024 + 128), jnp.int32)],
+        compiler_params=pltpu.CompilerParams(vmem_limit_bytes=20 * 2**20),
         name="tiles",
-    )(lists[:, :, :EB], counts[:2, :EB], hl)
+    )(lists, counts, split)
     summed = pl.pallas_call(
         scatter_kernel,
         out_shape=jax.ShapeDtypeStruct((8, TR, TR), F32),
-        in_specs=[any_space],
+        in_specs=[vmem],
         out_specs=vmem,
         scratch_shapes=[
-            pltpu.VMEM((128, TR, TR), F32),
             pltpu.VMEM((2, 2, 8, TR, TR), F32),
             pltpu.VMEM((2, 2, 16, TR, TR), F32),
             pltpu.VMEM((2, 2, 8, TR, TR), F32),
@@ -429,12 +375,10 @@
             pltpu.VMEM((2, 2, 2, TR, TR), F32),
             pltpu.VMEM((2, 2, 4, TR, TR), F32),
             pltpu.VMEM((2, 2, 2, TR, TR), F32),
-            pltpu.VMEM((8, TR, TR), F32),
             dma((24,)),
             dma((24,)),
-            dma((8,)),
         ],
-        compiler_params=pltpu.CompilerParams(collective_id=1, has_side_effects=True, vmem_limit_bytes=limit),
+        compiler_params=pltpu.CompilerParams(collective_id=1, has_side_effects=True, vmem_limit_bytes=20 * 2**20),
         name="scatter",
     )(part)
     return parent_entries - summed

time: 175 us -> 160 us (0.914)
  Pallas kernels: 169 us -> 154 us
    pallas_call x1, Pallas kernels: 41 us -> 27.4 us  [per_device(): pl.pallas_call(tiles_kernel, out_shape=jax.ShapeDtypeStruct((129, TR, TR)...]
    unnamed x2 -> x8, local copies, waits for them, and re-layouts: 0.01 us -> 3.19 us
    pallas_call x1, Pallas kernels: 82.2 us -> 79.7 us  [per_device(): pl.pallas_call(gather_kernel, out_shape=(jax.ShapeDtypeStruct((2, EB, 2 *...]
    broadcast_in_dim x2 -> x0, local copies, waits for them, and re-layouts: 1.97 us -> none  [the longest x1 1.37 us: per_device(): live = jnp.broadcast_to(tile_counts[:, None, None], (16, 8, 128))]
where the time goes in v2:
time: 160 us; the launch traced here: 158 us
  Pallas kernels  154 us (96%)
  local copies, waits for them, and re-layouts  3.19 us (2%)
    pallas_call x1, Pallas kernels, per_device(): pl.pallas_call(gather_kernel, out_shape=(jax.ShapeDtypeStruct((2, EB, 2 *...  79.7 us
    pallas_call x1, Pallas kernels, per_device(): pl.pallas_call(scatter_kernel, out_shape=jax.ShapeDtypeStruct((8, TR, TR)...  46.6 us
    pallas_call x1, Pallas kernels, per_device(): pl.pallas_call(tiles_kernel, out_shape=jax.ShapeDtypeStruct((129, TR, TR)...  27.4 us

profile of v2, /device:TPU:1, one launch (start us, length us, event | category | flops | bytes accessed | tf_op | source)
XLA Modules:
  0.0 158.4 jit_solution(5087070297752743934)
XLA Ops:
  0.7 0.0 copy-start
  0.7 1.6 copy-done
  2.2 0.0 copy-start.1
  2.2 0.9 copy-done.1
  3.2 0.0 copy-start.2
  3.2 0.7 copy-done.2
  3.9 79.7 %gather.1 = (bf16[2,32,256,512]{3,2,1,0:T(8,128)(2,1)S(1)}, s32[2,32,128]{2,1,0:T(8,128)S(1)}, s32[8,128]{1,0:T(8,128)S(1)}) custom-call(f32[512,1024]{1,0:T(8,128)S(1)} %bitcast.1, s32[16,32,32]{2,1,0:T(8,128)S(1)} %copy-done.1, s32[1]{0:T(128)S(6)} %copy.6.sizes, s32[16]{0:T(128)S(1)} %copy-done.2), custom_call_target="tpu_custom_call" | custom-call | tf_op jit(solution)/shard_map/gather/pallas_call | solution.py:331
  83.6 27.4 %tiles.1.part = f32[129,128,128]{2,1,0:T(8,128)S(1)} custom-call(s32[2,32,128]{2,1,0:T(8,128)S(1)} %get-tuple-element.8.lists, s32[8,128]{1,0:T(8,128)S(1)} %get-tuple-element.9.counts, bf16[2,32,256,512]{3,2,1,0:T(8,128)(2,1)S(1)} %get-tuple-element.10.held), custom_call_target="tpu_custom_call" | custom-call | tf_op jit(solution)/shard_map/tiles/pallas_call | solution.py:356
  111.0 0.0 copy-start.3
  111.0 46.6 %scatter.1 = f32[8,128,128]{2,1,0:T(8,128)S(1)} custom-call(f32[129,128,128]{2,1,0:T(8,128)S(1)} %tiles.1.part), custom_call_target="tpu_custom_call" | custom-call | tf_op jit(solution)/shard_map/scatter/pallas_call | solution.py:365
  157.5 0.0 copy-done.3
  157.5 0.9 sub.3
Async XLA Ops:
  0.7 1.6 %copy-start = (f32[1,512,1024]{2,1,0:T(8,128)S(1)}, f32[1,512,1024]{2,1,0:T(8,128)}, u32[]{:S(2)}) copy-start(f32[1,512,1024]{2,1,0:T(8,128)} %param.5) | copy-start | bytes 6291460
  2.2 0.9 copy-start.1
  3.2 0.7 copy-start.2
  111.0 46.6 %copy-start.3 = (f32[8,128,128]{2,1,0:T(8,128)S(1)}, f32[8,128,128]{2,1,0:T(8,128)}, u32[]{:S(2)}) copy-start(f32[8,128,128]{2,1,0:T(8,128)} %param.9) | copy-start | bytes 1572868

commit v3 on v2

--- a/solution.py
+++ b/solution.py
@@ -11,7 +11,11 @@
 KH = 512
 CB = 4
 EB = 32
-UNROLL = 16
+UNROLL = 8
+BATCH = 16
+FIXED = 32
+REST = 256
+TRASH = 128
 
 MESH = pl.DeviceIdType.MESH
 F32 = jnp.float32
@@ -41,8 +45,8 @@
 
 
 def gather_kernel(
-    x, parents, sizes, counts, split, lists, tile_counts,
-    mine, other, fs, fs_other,
+    x, parents, sizes, counts, split, staged, codes, rest, totals,
+    mine, other, fs, fs_other, targets, size_s, count_s, code_s, rows_by_place,
     x_send, z_send, recv, core_send, core_recv, local, fs_sem,
 ):
     p = position()
@@ -51,7 +55,15 @@
     across = device(p, xh=1 - xh)
     twin = device(p, core=1 - p["core"])
 
-    fs[...] = jnp.full((8, KH), sizes[0], jnp.int32)
+    fronts = [(p["front"] // 2) * 2 + (p["core"] if g == 0 else 1 - p["core"]) for g in range(2)]
+    small = [
+        pltpu.make_async_copy(sizes, size_s, local.at[4]),
+        pltpu.make_async_copy(counts, count_s, local.at[5]),
+        pltpu.make_async_copy(parents.at[fronts[0]], targets.at[0], local.at[6]),
+        pltpu.make_async_copy(parents.at[fronts[1]], targets.at[1], local.at[7]),
+    ]
+    for copy in small:
+        copy.start()
     barrier = pltpu.get_barrier_semaphore()
     for other_dev in (up, down, across, twin):
         pl.semaphore_signal(barrier, inc=1, device_id=other_dev, device_id_type=MESH)
@@ -94,8 +106,8 @@
     def rows(c):
         return pl.ds(c * TR, TR)
 
-    send(fs, fs_other, fs_sem.at[0], fs_sem.at[1], twin)
-    fs_copy = sent[-1]
+    small[0].wait()
+    fs[...] = jnp.full((8, KH), size_s[0], jnp.int32)
     loads = []
     for c in (0, 2, 1, 3):
         s = slot(1, 0, c)
@@ -107,17 +119,53 @@
         load.start()
         loads.append(load)
 
+    for copy in small[1:]:
+        copy.wait()
+    send(fs, fs_other, fs_sem.at[0], fs_sem.at[1], twin)
+    fs_copy = sent[-1]
+
     col = lax.broadcasted_iota(jnp.int32, (EB, EB), 1)
     row = lax.broadcasted_iota(jnp.int32, (EB, EB), 0)
     lower = (row >= col).astype(F32)
+    before = (row < col).astype(F32)
 
     def place_of(block):
         return ((((block >> 4) ^ xh) << 4) + ((((block >> 2) - z) & 3) << 2)) + (block & 3)
 
-    for g in range(2):
-        f = (p["front"] // 2) * 2 + (p["core"] if g == 0 else 1 - p["core"])
-        target = parents[f]
-        live = counts[f]
+    def level_of(s):
+        return jnp.where(s < 20, 0, jnp.where((s >= 24) & (s < 28), 2, 1))
+
+    a_slot, b_slot = place_of(row), place_of(col)
+    level = jnp.maximum(level_of(a_slot), level_of(b_slot))
+
+    def places(hit):
+        rank = jnp.dot(lower, hit.astype(F32), preferred_element_type=F32)
+        many = jnp.broadcast_to(rank[EB - 1 : EB, :], (8, EB))
+        start = jnp.dot(many, before, preferred_element_type=F32)
+        at = (rank + start[0:1, :]).astype(jnp.int32) - 1
+        return jnp.where(hit, at, -1), jnp.sum(many[0:1, :], axis=1, keepdims=True).astype(jnp.int32)
+
+    ones = jnp.full((8, EB), 1.0, F32)
+
+    def listed(at, code, size):
+        def eight(i, _):
+            first = pl.multiple_of(i * 8, 8)
+            for k in range(8):
+                rows_by_place[pl.ds(first + k, 1), 0:EB] = jnp.sum(
+                    jnp.where(at == first + k, code, 0.0), axis=0, keepdims=True
+                )
+            return 0
+
+        lax.fori_loop(0, size // 8, eight, 0)
+        found = lax.dot_general(
+            ones, rows_by_place[0:size, 0:EB], (((1,), (1,)), ((), ())),
+            precision=lax.Precision.HIGHEST, preferred_element_type=F32,
+        )
+        return found[0:1, :].astype(jnp.int32)
+
+    def plan(g):
+        target = targets[g]
+        live = count_s[fronts[g]]
         dest = target >> 3
         dest_front, dest_blk = dest >> 3, dest & 7
         hit = ((dest_blk & 3) == z) & ((dest_front & 1) == p["core"])
@@ -127,12 +175,30 @@
         place = target & 7
         first = place < 4
         at = jnp.where(first, ry * 4 + rx, 16 + rx * 4 + ry) * 4 + (place & 3)
-        code = (place_of(col) << 13) + (place_of(row) << 8) + at
-        rank = jnp.dot(lower, hit.astype(F32), preferred_element_type=F32).astype(jnp.int32)
-        tile_counts[g : g + 1, 0:EB] = rank[EB - 1 : EB, :]
-        rank = jnp.where(hit, rank, 0)
-        for k in range(EB):
-            lists[g, k : k + 1, 0:EB] = jnp.sum(jnp.where(rank == k + 1, code, 0), axis=0, keepdims=True)
+        code = ((b_slot << 13) + (a_slot << 8) + at).astype(F32)
+        over = level == 2
+        for n in range(2):
+            where, many = places(hit & (level == n))
+            codes[g * 2 + n : g * 2 + n + 1, 0:FIXED] = listed(where, code, FIXED)
+            totals[g * 2 + n : g * 2 + n + 1, :] = jnp.broadcast_to(many, (1, 128))
+            over = over | (where >= FIXED)
+        where, many = places(hit & over)
+        rest[g : g + 1, :] = listed(where, code, REST)
+        totals[4 + g : 5 + g, :] = jnp.broadcast_to(many, (1, 128))
+
+    def products(g, n, first, steps):
+        def step(i, _):
+            for u in range(BATCH):
+                t = (first + i) * BATCH + u
+                c = code_s[g * 2 + n, t]
+                d = lax.dot_general(
+                    split[g, (c >> 8) & 31], split[g, (c >> 13) & 31], (((1,), (1,)), ((), ())),
+                    preferred_element_type=F32,
+                )
+                staged[g, n * FIXED + t] = d[:TR, :TR] + (d[:TR, TR:] + d[TR:, :TR])
+            return 0
+
+        lax.fori_loop(0, steps, step, 0)
 
     def convert(g, s):
         src = mine if g == 0 else other
@@ -164,6 +230,7 @@
         from_twin(t)
         convert(1, t)
 
+    plan(0)
     fs_copy.wait_recv()
     for c, load in zip((0, 1, 2, 3), loads):
         load.wait()
@@ -184,10 +251,19 @@
         send_z(mine.at[s], 1, 3, e, up)
         send_z(mine.at[s], 1, 1, e, down)
         take(s)
+        if i == 0:
+            plan(1)
+        if i == 2:
+            code_copy = pltpu.make_async_copy(codes, code_s, local.at[8])
+            code_copy.start()
     for e in (0, 2, 1, 3):
         arrived(slot(0, 2, e))
         take(slot(0, 2, e))
-    for e in (0, 2, 1, 3):
+    code_copy.wait()
+    while twin_queue:
+        drain()
+    work = [(0, 0), (1, 0), (0, 1), (1, 1)]
+    for e, many in zip((0, 2, 1, 3), (1, 1, 1, 1)):
         s = slot(1, 3, e)
         arrived(s)
         if e < 2:
@@ -198,7 +274,17 @@
         if e >= 2:
             send_z(mine.at[s], 1, 2, e, down)
         take(s)
-    for e in (0, 2, 1, 3):
+        for _ in range(many):
+            g, first = work.pop(0)
+            products(g, 0, first, 1)
+    while twin_queue:
+        drain()
+    products(0, 1, 0, 2)
+    for e in (0, 2):
+        arrived(slot(1, 2, e))
+        take(slot(1, 2, e))
+    products(1, 1, 0, 2)
+    for e in (1, 3):
         arrived(slot(1, 2, e))
         take(slot(1, 2, e))
     while twin_queue:
@@ -207,39 +293,46 @@
         copy.wait_send()
 
 
-def tiles_kernel(lists, counts, held, acc, flat):
+def tiles_kernel(codes, rest, totals, held, staged, acc, flat):
     def clear(i, _):
         acc[i] = jnp.zeros((TR, TR), F32)
         return 0
 
-    lax.fori_loop(0, 129, clear, 0)
-
-    totals = []
+    lax.fori_loop(0, TRASH + 1, clear, 0)
     for g in range(2):
-        def column(b, n):
-            def entry(k, n):
-                flat[g, n] = lists[g, k, b]
-                return n + 1
-
-            return lax.fori_loop(0, counts[g, b], entry, n)
-
-        n = lax.fori_loop(0, EB, column, 0)
-        for u in range(UNROLL - 1):
-            flat[g, n + u] = 128
-        totals.append(n)
-
+        for n in range(2):
+            many = totals[g * 2 + n, 0]
+
+            def add(i, _):
+                for u in range(8):
+                    t = i * 8 + u
+                    at = jnp.where(t < many, codes[g * 2 + n, t] & 255, TRASH)
+                    acc[at] += staged[g, n * FIXED + t]
+                return 0
+
+            lax.fori_loop(0, FIXED // 8, add, 0)
+    count = 0
     for g in range(2):
-        def several(i, _):
-            for u in range(UNROLL):
-                code = flat[g, i * UNROLL + u]
-                b, a, at = code >> 13, (code >> 8) & 31, code & 255
-                d = lax.dot_general(
-                    held[g, a], held[g, b], (((1,), (1,)), ((), ())), preferred_element_type=F32
-                )
-                acc[at] += d[:TR, :TR] + (d[:TR, TR:] + d[TR:, :TR])
+        def entry(k, _):
+            flat[count + k] = rest[g, k] + (g << 18)
             return 0
 
-        lax.fori_loop(0, (totals[g] + UNROLL - 1) // UNROLL, several, 0)
+        lax.fori_loop(0, totals[4 + g, 0], entry, 0)
+        count = count + totals[4 + g, 0]
+    for u in range(UNROLL - 1):
+        flat[count + u] = TRASH
+
+    def several(i, _):
+        for u in range(UNROLL):
+            c = flat[i * UNROLL + u]
+            g, b, a, at = c >> 18, (c >> 13) & 31, (c >> 8) & 31, c & 255
+            d = lax.dot_general(
+                held[g, a], held[g, b], (((1,), (1,)), ((), ())), preferred_element_type=F32
+            )
+            acc[at] += d[:TR, :TR] + (d[:TR, TR:] + d[TR:, :TR])
+        return 0
+
+    lax.fori_loop(0, (count + UNROLL - 1) // UNROLL, several, 0)
 
 
 def scatter_kernel(
@@ -324,44 +417,51 @@
 
 
 def per_device(factor_rows, front_sizes, tile_counts, parent_tiles, parent_entries):
-    any_space = pl.BlockSpec(memory_space=pl.ANY)
     vmem = pl.BlockSpec(memory_space=pltpu.VMEM)
     smem = pl.BlockSpec(memory_space=pltpu.SMEM)
     dma = pltpu.SemaphoreType.DMA
-    split, lists, counts = pl.pallas_call(
+    hbm = pl.BlockSpec(memory_space=pltpu.HBM)
+    split, staged, codes, rest, totals = pl.pallas_call(
         gather_kernel,
         out_shape=(
             jax.ShapeDtypeStruct((2, EB, 2 * TR, KH), BF16),
-            jax.ShapeDtypeStruct((2, EB, 128), jnp.int32),
+            jax.ShapeDtypeStruct((2, 2 * FIXED, TR, TR), F32),
+            jax.ShapeDtypeStruct((8, 128), jnp.int32),
+            jax.ShapeDtypeStruct((8, REST), jnp.int32),
             jax.ShapeDtypeStruct((8, 128), jnp.int32),
         ),
-        in_specs=[any_space, vmem, smem, smem],
-        out_specs=(vmem, vmem, vmem),
+        in_specs=[hbm, hbm, hbm, hbm],
+        out_specs=(vmem, vmem, vmem, vmem, vmem),
         scratch_shapes=[
             pltpu.VMEM((EB, TR, KH), F32),
             pltpu.VMEM((EB, TR, KH), F32),
             pltpu.VMEM((8, KH), jnp.int32),
             pltpu.VMEM((8, KH), jnp.int32),
+            pltpu.VMEM((2, EB, EB), jnp.int32),
+            pltpu.SMEM((1,), jnp.int32),
+            pltpu.SMEM((16,), jnp.int32),
+            pltpu.SMEM((8, 128), jnp.int32),
+            pltpu.VMEM((REST, 128), F32),
             dma((4,)),
             dma((24,)),
             dma((32,)),
             dma((32,)),
             dma((32,)),
-            dma((4,)),
+            dma((9,)),
             dma((2,)),
         ],
-        compiler_params=pltpu.CompilerParams(collective_id=0, has_side_effects=True, vmem_limit_bytes=20 * 2**20),
+        compiler_params=pltpu.CompilerParams(collective_id=0, has_side_effects=True, vmem_limit_bytes=18 * 2**20),
         name="gather",
     )(factor_rows[0], parent_tiles, front_sizes, tile_counts)
     part = pl.pallas_call(
         tiles_kernel,
-        out_shape=jax.ShapeDtypeStruct((129, TR, TR), F32),
-        in_specs=[smem, smem, vmem],
+        out_shape=jax.ShapeDtypeStruct((TRASH + 1, TR, TR), F32),
+        in_specs=[smem, smem, smem, vmem, vmem],
         out_specs=vmem,
-        scratch_shapes=[pltpu.SMEM((2, 1024 + 128), jnp.int32)],
-        compiler_params=pltpu.CompilerParams(vmem_limit_bytes=20 * 2**20),
+        scratch_shapes=[pltpu.SMEM((2 * REST + UNROLL,), jnp.int32)],
+        compiler_params=pltpu.CompilerParams(vmem_limit_bytes=4 * 2**20),
         name="tiles",
-    )(lists, counts, split)
+    )(codes, rest, totals, split, staged)
     summed = pl.pallas_call(
         scatter_kernel,
         out_shape=jax.ShapeDtypeStruct((8, TR, TR), F32),
@@ -378,7 +478,7 @@
             dma((24,)),
             dma((24,)),
         ],
-        compiler_params=pltpu.CompilerParams(collective_id=1, has_side_effects=True, vmem_limit_bytes=20 * 2**20),
+        compiler_params=pltpu.CompilerParams(collective_id=1, has_side_effects=True, vmem_limit_bytes=14 * 2**20),
         name="scatter",
     )(part)
     return parent_entries - summed

time: 160 us -> 149 us (0.931)
  Pallas kernels: 154 us -> 144 us
    pallas_call x1, Pallas kernels: 27.4 us -> 15 us  [per_device(): pl.pallas_call(tiles_kernel, out_shape=jax.ShapeDtypeStruct((TRASH + 1, T...]
    pallas_call x1, Pallas kernels: 46.6 us -> 49.6 us  [per_device(): pl.pallas_call(scatter_kernel, out_shape=jax.ShapeDtypeStruct((8, TR, TR)...]
where the time goes in v3:
time: 149 us
  Pallas kernels  144 us (97%)
  local copies, waits for them, and re-layouts  3.19 us (2%)
    pallas_call x1, Pallas kernels, per_device(): pl.pallas_call(gather_kernel, out_shape=(jax.ShapeDtypeStruct((2, EB, 2 *...  79.2 us
    pallas_call x1, Pallas kernels, per_device(): pl.pallas_call(scatter_kernel, out_shape=jax.ShapeDtypeStruct((8, TR, TR)...  49.6 us
    pallas_call x1, Pallas kernels, per_device(): pl.pallas_call(tiles_kernel, out_shape=jax.ShapeDtypeStruct((TRASH + 1, T...  15 us
    unnamed x8, local copies, waits for them, and re-layouts  3.19 us

profile of v3, /device:TPU:1, one launch (start us, length us, event | category | flops | bytes accessed | tf_op | source)
XLA Modules:
  0.0 148.7 jit_solution(14141948578308604313)
XLA Ops:
  0.7 0.0 copy-start
  0.7 1.6 %copy-done = f32[1,512,1024]{2,1,0:T(8,128)S(1)} copy-done((f32[1,512,1024]{2,1,0:T(8,128)S(1)}, f32[1,512,1024]{2,1,0:T(8,128)}, u32[]{:S(2)}) %copy-start) | copy-done | bytes 2097176
  2.2 0.0 copy-start.1
  2.2 0.9 copy-done.1
  3.2 0.0 copy-start.2
  3.2 0.7 copy-done.2
  3.9 79.2 %gather.1 = (bf16[2,32,256,512]{3,2,1,0:T(8,128)(2,1)S(1)}, f32[2,64,128,128]{3,2,1,0:T(8,128)S(1)}, s32[8,128]{1,0:T(8,128)S(1)}, s32[8,256]{1,0:T(8,128)S(1)}, s32[8,128]{1,0:T(8,128)S(1)}) custom-call(f32[512,1024]{1,0:T(8,128)S(1)} %bitcast.1, s32[16,32,32]{2,1,0:T(8,128)S(1)} %copy-done.1, s32[1]{0:T(128)S(6)} %copy.6.sizes, s32[16]{0:T(128)S(1)} %copy-done.2), custom_call_target="tpu_custom_call" | custom-call | tf_op jit(solution)/shard_map/gather/pallas_call | solution.py:424
  83.1 15.0 %tiles.1.part = f32[129,128,128]{2,1,0:T(8,128)S(1)} custom-call(s32[8,128]{1,0:T(8,128)S(1)} %get-tuple-element.10.codes, s32[8,256]{1,0:T(8,128)S(1)} %get-tuple-element.11.rest, s32[8,128]{1,0:T(8,128)S(1)} %get-tuple-element.12.totals, bf16[2,32,256,512]{3,2,1,0:T(8,128)(2,1)S(1)} %get-tuple-element.13.held, f32[2,64,128,128]{3,2,1,0:T(8,128)S(1)} %get-tuple-element.14.staged), custom_call_target="tpu_custom_call" | custom-call | tf_op jit(solution)/shard_map/tiles/pallas_call | solution.py:456
  98.1 0.0 copy-start.3
  98.2 49.6 %scatter.1 = f32[8,128,128]{2,1,0:T(8,128)S(1)} custom-call(f32[129,128,128]{2,1,0:T(8,128)S(1)} %tiles.1.part), custom_call_target="tpu_custom_call" | custom-call | tf_op jit(solution)/shard_map/scatter/pallas_call | solution.py:465
  147.8 0.0 copy-done.3
  147.8 0.9 sub.3
Async XLA Ops:
  0.7 1.6 %copy-start = (f32[1,512,1024]{2,1,0:T(8,128)S(1)}, f32[1,512,1024]{2,1,0:T(8,128)}, u32[]{:S(2)}) copy-start(f32[1,512,1024]{2,1,0:T(8,128)} %param.5) | copy-start | bytes 6291460
  2.2 0.9 copy-start.1
  3.2 0.7 copy-start.2
  98.1 49.7 %copy-start.3 = (f32[8,128,128]{2,1,0:T(8,128)S(1)}, f32[8,128,128]{2,1,0:T(8,128)}, u32[]{:S(2)}) copy-start(f32[8,128,128]{2,1,0:T(8,128)} %param.9) | copy-start | bytes 1572868

commit v4 on v3

--- a/solution.py
+++ b/solution.py
@@ -13,7 +13,9 @@
 EB = 32
 UNROLL = 8
 BATCH = 16
-FIXED = 32
+FIXED = (48, 48, 16)
+REUSED = 40
+FREED = (20, 21, 22, 23, 28, 29, 30, 31)
 REST = 256
 TRASH = 128
 
@@ -45,8 +47,8 @@
 
 
 def gather_kernel(
-    x, parents, sizes, counts, split, staged, codes, rest, totals,
-    mine, other, fs, fs_other, targets, size_s, count_s, code_s, rows_by_place,
+    x, parents, sizes, counts, split, other, staged, codes, rest, totals,
+    mine, fs, fs_other, targets, count_s, code_s, rows_by_place,
     x_send, z_send, recv, core_send, core_recv, local, fs_sem,
 ):
     p = position()
@@ -57,7 +59,6 @@
 
     fronts = [(p["front"] // 2) * 2 + (p["core"] if g == 0 else 1 - p["core"]) for g in range(2)]
     small = [
-        pltpu.make_async_copy(sizes, size_s, local.at[4]),
         pltpu.make_async_copy(counts, count_s, local.at[5]),
         pltpu.make_async_copy(parents.at[fronts[0]], targets.at[0], local.at[6]),
         pltpu.make_async_copy(parents.at[fronts[1]], targets.at[1], local.at[7]),
@@ -106,8 +107,7 @@
     def rows(c):
         return pl.ds(c * TR, TR)
 
-    small[0].wait()
-    fs[...] = jnp.full((8, KH), size_s[0], jnp.int32)
+    fs[...] = jnp.full((8, KH), sizes[0], jnp.int32)
     loads = []
     for c in (0, 2, 1, 3):
         s = slot(1, 0, c)
@@ -119,7 +119,7 @@
         load.start()
         loads.append(load)
 
-    for copy in small[1:]:
+    for copy in small:
         copy.wait()
     send(fs, fs_other, fs_sem.at[0], fs_sem.at[1], twin)
     fs_copy = sent[-1]
@@ -133,7 +133,7 @@
         return ((((block >> 4) ^ xh) << 4) + ((((block >> 2) - z) & 3) << 2)) + (block & 3)
 
     def level_of(s):
-        return jnp.where(s < 20, 0, jnp.where((s >= 24) & (s < 28), 2, 1))
+        return jnp.where(s < 20, 0, jnp.where((s >= 24) & (s < 28), 2 + (s & 1), 1))
 
     a_slot, b_slot = place_of(row), place_of(col)
     level = jnp.maximum(level_of(a_slot), level_of(b_slot))
@@ -176,29 +176,42 @@
         first = place < 4
         at = jnp.where(first, ry * 4 + rx, 16 + rx * 4 + ry) * 4 + (place & 3)
         code = ((b_slot << 13) + (a_slot << 8) + at).astype(F32)
-        over = level == 2
-        for n in range(2):
+        over = level == 3
+        for n in range(3):
             where, many = places(hit & (level == n))
-            codes[g * 2 + n : g * 2 + n + 1, 0:FIXED] = listed(where, code, FIXED)
-            totals[g * 2 + n : g * 2 + n + 1, :] = jnp.broadcast_to(many, (1, 128))
-            over = over | (where >= FIXED)
+            codes[g * 4 + n : g * 4 + n + 1, 0 : FIXED[n]] = listed(where, code, FIXED[n])
+            totals[g * 4 + n : g * 4 + n + 1, :] = jnp.broadcast_to(many, (1, 128))
+            over = over | (where >= FIXED[n])
         where, many = places(hit & over)
         rest[g : g + 1, :] = listed(where, code, REST)
-        totals[4 + g : 5 + g, :] = jnp.broadcast_to(many, (1, 128))
-
-    def products(g, n, first, steps):
+        totals[g * 4 + 3 : g * 4 + 4, :] = jnp.broadcast_to(many, (1, 128))
+
+    def product(g, n, t):
+        c = code_s[g * 4 + n, t]
+        d = lax.dot_general(
+            split[g, (c >> 8) & 31], split[g, (c >> 13) & 31], (((1,), (1,)), ((), ())),
+            preferred_element_type=F32,
+        )
+        return d[:TR, :TR] + (d[:TR, TR:] + d[TR:, :TR])
+
+    def products(g, n, first):
+        for t in range(first * BATCH, (first + 1) * BATCH):
+            lanes = pl.ds((t % 4) * TR, TR)
+            if n == 2:
+                other[FREED[g * 4 + t // 4], :, lanes] = product(g, n, t)
+            elif t < REUSED:
+                other[g * 10 + t // 4, :, lanes] = product(g, n, t)
+            else:
+                staged[g, t - REUSED] = product(g, n, t)
+
+    def products_1(g):
         def step(i, _):
             for u in range(BATCH):
-                t = (first + i) * BATCH + u
-                c = code_s[g * 2 + n, t]
-                d = lax.dot_general(
-                    split[g, (c >> 8) & 31], split[g, (c >> 13) & 31], (((1,), (1,)), ((), ())),
-                    preferred_element_type=F32,
-                )
-                staged[g, n * FIXED + t] = d[:TR, :TR] + (d[:TR, TR:] + d[TR:, :TR])
+                t = i * BATCH + u
+                staged[g, FIXED[0] - REUSED + t] = product(g, 1, t)
             return 0
 
-        lax.fori_loop(0, steps, step, 0)
+        lax.fori_loop(0, FIXED[1] // BATCH, step, 0)
 
     def convert(g, s):
         src = mine if g == 0 else other
@@ -262,8 +275,8 @@
     code_copy.wait()
     while twin_queue:
         drain()
-    work = [(0, 0), (1, 0), (0, 1), (1, 1)]
-    for e, many in zip((0, 2, 1, 3), (1, 1, 1, 1)):
+    work = [(0, 0), (1, 0), (0, 1), (1, 1), (0, 2), (1, 2)]
+    for e, many in zip((0, 2, 1, 3), (2, 2, 1, 1)):
         s = slot(1, 3, e)
         arrived(s)
         if e < 2:
@@ -276,49 +289,63 @@
         take(s)
         for _ in range(many):
             g, first = work.pop(0)
-            products(g, 0, first, 1)
+            products(g, 0, first)
     while twin_queue:
         drain()
-    products(0, 1, 0, 2)
+    products_1(0)
     for e in (0, 2):
         arrived(slot(1, 2, e))
         take(slot(1, 2, e))
-    products(1, 1, 0, 2)
+    products_1(1)
+    while twin_queue:
+        drain()
+    products(0, 2, 0)
     for e in (1, 3):
         arrived(slot(1, 2, e))
         take(slot(1, 2, e))
+    products(1, 2, 0)
     while twin_queue:
         drain()
     for copy in sent:
         copy.wait_send()
 
 
-def tiles_kernel(codes, rest, totals, held, staged, acc, flat):
+def tiles_kernel(codes, rest, totals, held, reused, staged, acc, flat):
     def clear(i, _):
         acc[i] = jnp.zeros((TR, TR), F32)
         return 0
 
     lax.fori_loop(0, TRASH + 1, clear, 0)
+    def add(g, n, t, value):
+        at = jnp.where(t < totals[g * 4 + n, 0], codes[g * 4 + n, t] & 255, TRASH)
+        acc[at] += value
+
     for g in range(2):
-        for n in range(2):
-            many = totals[g * 2 + n, 0]
-
-            def add(i, _):
-                for u in range(8):
-                    t = i * 8 + u
-                    at = jnp.where(t < many, codes[g * 2 + n, t] & 255, TRASH)
-                    acc[at] += staged[g, n * FIXED + t]
-                return 0
-
-            lax.fori_loop(0, FIXED // 8, add, 0)
+        def four(i, _):
+            for u in range(4):
+                add(g, 0, i * 4 + u, reused[g * 10 + i, :, pl.ds(u * TR, TR)])
+            return 0
+
+        lax.fori_loop(0, REUSED // 4, four, 0)
+        for t in range(REUSED, FIXED[0]):
+            add(g, 0, t, staged[g, t - REUSED])
+
+        def eight(i, _):
+            for u in range(8):
+                add(g, 1, i * 8 + u, staged[g, FIXED[0] - REUSED + i * 8 + u])
+            return 0
+
+        lax.fori_loop(0, FIXED[1] // 8, eight, 0)
+        for t in range(FIXED[2]):
+            add(g, 2, t, reused[FREED[g * 4 + t // 4], :, pl.ds((t % 4) * TR, TR)])
     count = 0
     for g in range(2):
         def entry(k, _):
             flat[count + k] = rest[g, k] + (g << 18)
             return 0
 
-        lax.fori_loop(0, totals[4 + g, 0], entry, 0)
-        count = count + totals[4 + g, 0]
+        lax.fori_loop(0, totals[g * 4 + 3, 0], entry, 0)
+        count = count + totals[g * 4 + 3, 0]
     for u in range(UNROLL - 1):
         flat[count + u] = TRASH
 
@@ -421,24 +448,27 @@
     smem = pl.BlockSpec(memory_space=pltpu.SMEM)
     dma = pltpu.SemaphoreType.DMA
     hbm = pl.BlockSpec(memory_space=pltpu.HBM)
-    split, staged, codes, rest, totals = pl.pallas_call(
+
+    def in_hbm(a):
+        return pltpu.with_memory_space_constraint(a, pltpu.HBM)
+
+    split, reused, staged, codes, rest, totals = pl.pallas_call(
         gather_kernel,
         out_shape=(
             jax.ShapeDtypeStruct((2, EB, 2 * TR, KH), BF16),
-            jax.ShapeDtypeStruct((2, 2 * FIXED, TR, TR), F32),
+            jax.ShapeDtypeStruct((EB, TR, KH), F32),
+            jax.ShapeDtypeStruct((2, FIXED[0] - REUSED + FIXED[1], TR, TR), F32),
             jax.ShapeDtypeStruct((8, 128), jnp.int32),
             jax.ShapeDtypeStruct((8, REST), jnp.int32),
             jax.ShapeDtypeStruct((8, 128), jnp.int32),
         ),
-        in_specs=[hbm, hbm, hbm, hbm],
-        out_specs=(vmem, vmem, vmem, vmem, vmem),
+        in_specs=[hbm, hbm, smem, hbm],
+        out_specs=(vmem,) * 6,
         scratch_shapes=[
-            pltpu.VMEM((EB, TR, KH), F32),
             pltpu.VMEM((EB, TR, KH), F32),
             pltpu.VMEM((8, KH), jnp.int32),
             pltpu.VMEM((8, KH), jnp.int32),
             pltpu.VMEM((2, EB, EB), jnp.int32),
-            pltpu.SMEM((1,), jnp.int32),
             pltpu.SMEM((16,), jnp.int32),
             pltpu.SMEM((8, 128), jnp.int32),
             pltpu.VMEM((REST, 128), F32),
@@ -450,18 +480,18 @@
             dma((9,)),
             dma((2,)),
         ],
-        compiler_params=pltpu.CompilerParams(collective_id=0, has_side_effects=True, vmem_limit_bytes=18 * 2**20),
+        compiler_params=pltpu.CompilerParams(collective_id=0, has_side_effects=True, vmem_limit_bytes=10 * 2**20),
         name="gather",
-    )(factor_rows[0], parent_tiles, front_sizes, tile_counts)
+    )(in_hbm(factor_rows[0]), in_hbm(parent_tiles), front_sizes, in_hbm(tile_counts))
     part = pl.pallas_call(
         tiles_kernel,
         out_shape=jax.ShapeDtypeStruct((TRASH + 1, TR, TR), F32),
-        in_specs=[smem, smem, smem, vmem, vmem],
+        in_specs=[smem, smem, smem, vmem, vmem, vmem],
         out_specs=vmem,
         scratch_shapes=[pltpu.SMEM((2 * REST + UNROLL,), jnp.int32)],
         compiler_params=pltpu.CompilerParams(vmem_limit_bytes=4 * 2**20),
         name="tiles",
-    )(codes, rest, totals, split, staged)
+    )(codes, rest, totals, split, reused, staged)
     summed = pl.pallas_call(
         scatter_kernel,
         out_shape=jax.ShapeDtypeStruct((8, TR, TR), F32),

time: 149 us -> 141 us (0.946)
  Pallas kernels: 144 us -> 138 us
  local copies, waits for them, and re-layouts: 3.19 us -> 0.01 us
    pallas_call x1, Pallas kernels: 15 us -> 8.53 us  [per_device(): pl.pallas_call(tiles_kernel, out_shape=jax.ShapeDtypeStruct((TRASH + 1, T...]
    unnamed x8 -> x2, local copies, waits for them, and re-layouts: 3.19 us -> 0.01 us
    pallas_call x1, Pallas kernels: 79.2 us -> 80.9 us  [per_device(): pl.pallas_call(gather_kernel, out_shape=(jax.ShapeDtypeStruct((2, EB, 2 *...]
where the time goes in v4:
time: 141 us; the launch traced here: 140 us
  Pallas kernels  138 us (98%)
    pallas_call x1, Pallas kernels, per_device(): pl.pallas_call(gather_kernel, out_shape=(jax.ShapeDtypeStruct((2, EB, 2 *...  80.9 us
    pallas_call x1, Pallas kernels, per_device(): pl.pallas_call(scatter_kernel, out_shape=jax.ShapeDtypeStruct((8, TR, TR)...  48.8 us
    pallas_call x1, Pallas kernels, per_device(): pl.pallas_call(tiles_kernel, out_shape=jax.ShapeDtypeStruct((TRASH + 1, T...  8.53 us

profile of v4, /device:TPU:1, one launch (start us, length us, event | category | flops | bytes accessed | tf_op | source)
XLA Modules:
  0.0 139.7 jit_solution(3701909818454963811)
XLA Ops:
  0.7 80.9 %gather.1 = (bf16[2,32,256,512]{3,2,1,0:T(8,128)(2,1)S(1)}, f32[32,128,512]{2,1,0:T(8,128)S(1)}, f32[2,56,128,128]{3,2,1,0:T(8,128)S(1)}, s32[8,128]{1,0:T(8,128...) custom-call(f32[512,1024]{1,0:T(8,128)} %bitcast.1, s32[16,32,32]{2,1,0:T(8,128)} %parents.1, s32[1]{0:T(128)S(6)} %copy.6.sizes, ...), custom_call_target="tpu_custom_call" | custom-call | tf_op jit(solution)/shard_map/gather/pallas_call | solution.py:455
  81.6 8.5 %tiles.1.part = f32[129,128,128]{2,1,0:T(8,128)S(1)} custom-call(s32[8,128]{1,0:T(8,128)S(1)} %get-tuple-element.11.codes, s32[8,256]{1,0:T(8,128)S(1)} %get-tuple-element.12.rest, s32[8,128]{1,0:T(8,128)S(1)} %get-tuple-element.13.totals, bf16[2,32,256,512]{3,2,1,0:T(8,128)(2,1)S(1)} %get-tuple-element.14.held, ...), custom_call_target="tpu_custom_call" | custom-call | tf_op jit(solution)/shard_map/tiles/pallas_call | solution.py:486
  90.1 0.0 copy-start
  90.1 48.8 %scatter.1 = f32[8,128,128]{2,1,0:T(8,128)S(1)} custom-call(f32[129,128,128]{2,1,0:T(8,128)S(1)} %tiles.1.part), custom_call_target="tpu_custom_call" | custom-call | tf_op jit(solution)/shard_map/scatter/pallas_call | solution.py:495
  138.9 0.0 copy-done
  138.9 0.9 sub.3
Async XLA Ops:
  90.1 48.8 %copy-start = (f32[8,128,128]{2,1,0:T(8,128)S(1)}, f32[8,128,128]{2,1,0:T(8,128)}, u32[]{:S(2)}) copy-start(f32[8,128,128]{2,1,0:T(8,128)} %param.9) | copy-start | bytes 1572868

commit v5 on v4

--- a/solution.py
+++ b/solution.py
@@ -13,9 +13,10 @@
 EB = 32
 UNROLL = 8
 BATCH = 16
-FIXED = (48, 48, 16)
+FIXED = (48, 24, 28, 16)
 REUSED = 40
 FREED = (20, 21, 22, 23, 28, 29, 30, 31)
+BEGIN = (0, 8, 32)
 REST = 256
 TRASH = 128
 
@@ -133,7 +134,7 @@
         return ((((block >> 4) ^ xh) << 4) + ((((block >> 2) - z) & 3) << 2)) + (block & 3)
 
     def level_of(s):
-        return jnp.where(s < 20, 0, jnp.where((s >= 24) & (s < 28), 2 + (s & 1), 1))
+        return jnp.where(s < 20, 0, jnp.where((s >= 24) & (s < 28), 3, 1) + (s & 1))
 
     a_slot, b_slot = place_of(row), place_of(col)
     level = jnp.maximum(level_of(a_slot), level_of(b_slot))
@@ -156,12 +157,13 @@
                 )
             return 0
 
-        lax.fori_loop(0, size // 8, eight, 0)
+        whole = (size + 7) // 8 * 8
+        lax.fori_loop(0, whole // 8, eight, 0)
         found = lax.dot_general(
-            ones, rows_by_place[0:size, 0:EB], (((1,), (1,)), ((), ())),
+            ones, rows_by_place[0:whole, 0:EB], (((1,), (1,)), ((), ())),
             precision=lax.Precision.HIGHEST, preferred_element_type=F32,
         )
-        return found[0:1, :].astype(jnp.int32)
+        return found[0:1, 0:size].astype(jnp.int32)
 
     def plan(g):
         target = targets[g]
@@ -176,15 +178,15 @@
         first = place < 4
         at = jnp.where(first, ry * 4 + rx, 16 + rx * 4 + ry) * 4 + (place & 3)
         code = ((b_slot << 13) + (a_slot << 8) + at).astype(F32)
-        over = level == 3
-        for n in range(3):
+        over = level == 4
+        for n in range(4):
             where, many = places(hit & (level == n))
             codes[g * 4 + n : g * 4 + n + 1, 0 : FIXED[n]] = listed(where, code, FIXED[n])
-            totals[g * 4 + n : g * 4 + n + 1, :] = jnp.broadcast_to(many, (1, 128))
+            totals[g * 8 + n : g * 8 + n + 1, :] = jnp.broadcast_to(many, (1, 128))
             over = over | (where >= FIXED[n])
         where, many = places(hit & over)
         rest[g : g + 1, :] = listed(where, code, REST)
-        totals[g * 4 + 3 : g * 4 + 4, :] = jnp.broadcast_to(many, (1, 128))
+        totals[g * 8 + 4 : g * 8 + 5, :] = jnp.broadcast_to(many, (1, 128))
 
     def product(g, n, t):
         c = code_s[g * 4 + n, t]
@@ -194,24 +196,15 @@
         )
         return d[:TR, :TR] + (d[:TR, TR:] + d[TR:, :TR])
 
-    def products(g, n, first):
-        for t in range(first * BATCH, (first + 1) * BATCH):
+    def products(g, n, begin, end):
+        for t in range(begin, end):
             lanes = pl.ds((t % 4) * TR, TR)
-            if n == 2:
+            if n == 3:
                 other[FREED[g * 4 + t // 4], :, lanes] = product(g, n, t)
-            elif t < REUSED:
+            elif n == 0 and t < REUSED:
                 other[g * 10 + t // 4, :, lanes] = product(g, n, t)
             else:
-                staged[g, t - REUSED] = product(g, n, t)
-
-    def products_1(g):
-        def step(i, _):
-            for u in range(BATCH):
-                t = i * BATCH + u
-                staged[g, FIXED[0] - REUSED + t] = product(g, 1, t)
-            return 0
-
-        lax.fori_loop(0, FIXED[1] // BATCH, step, 0)
+                staged[g, BEGIN[n] + t - (REUSED if n == 0 else 0)] = product(g, n, t)
 
     def convert(g, s):
         src = mine if g == 0 else other
@@ -276,7 +269,12 @@
     while twin_queue:
         drain()
     work = [(0, 0), (1, 0), (0, 1), (1, 1), (0, 2), (1, 2)]
-    for e, many in zip((0, 2, 1, 3), (2, 2, 1, 1)):
+
+    def batch():
+        g, first = work.pop(0)
+        products(g, 0, first * BATCH, (first + 1) * BATCH)
+
+    for e in (0, 2, 1, 3):
         s = slot(1, 3, e)
         arrived(s)
         if e < 2:
@@ -287,23 +285,30 @@
         if e >= 2:
             send_z(mine.at[s], 1, 2, e, down)
         take(s)
-        for _ in range(many):
-            g, first = work.pop(0)
-            products(g, 0, first)
+        if e in (0, 2):
+            batch()
+            batch()
+        if e == 2:
+            while twin_queue:
+                drain()
+            batch()
+            batch()
+        if e in (1, 3):
+            products(0 if e == 1 else 1, 1, 0, FIXED[1])
     while twin_queue:
         drain()
-    products_1(0)
+    products(0, 2, 0, FIXED[2])
     for e in (0, 2):
         arrived(slot(1, 2, e))
         take(slot(1, 2, e))
-    products_1(1)
+    products(1, 2, 0, FIXED[2])
     while twin_queue:
         drain()
-    products(0, 2, 0)
+    products(0, 3, 0, FIXED[3])
+    products(1, 3, 0, FIXED[3])
     for e in (1, 3):
         arrived(slot(1, 2, e))
         take(slot(1, 2, e))
-    products(1, 2, 0)
     while twin_queue:
         drain()
     for copy in sent:
@@ -317,7 +322,7 @@
 
     lax.fori_loop(0, TRASH + 1, clear, 0)
     def add(g, n, t, value):
-        at = jnp.where(t < totals[g * 4 + n, 0], codes[g * 4 + n, t] & 255, TRASH)
+        at = jnp.where(t < totals[g * 8 + n, 0], codes[g * 4 + n, t] & 255, TRASH)
         acc[at] += value
 
     for g in range(2):
@@ -330,22 +335,23 @@
         for t in range(REUSED, FIXED[0]):
             add(g, 0, t, staged[g, t - REUSED])
 
-        def eight(i, _):
-            for u in range(8):
-                add(g, 1, i * 8 + u, staged[g, FIXED[0] - REUSED + i * 8 + u])
-            return 0
-
-        lax.fori_loop(0, FIXED[1] // 8, eight, 0)
-        for t in range(FIXED[2]):
-            add(g, 2, t, reused[FREED[g * 4 + t // 4], :, pl.ds((t % 4) * TR, TR)])
+        for n in (1, 2):
+            def some(i, _):
+                for u in range(4):
+                    add(g, n, i * 4 + u, staged[g, BEGIN[n] + i * 4 + u])
+                return 0
+
+            lax.fori_loop(0, FIXED[n] // 4, some, 0)
+        for t in range(FIXED[3]):
+            add(g, 3, t, reused[FREED[g * 4 + t // 4], :, pl.ds((t % 4) * TR, TR)])
     count = 0
     for g in range(2):
         def entry(k, _):
             flat[count + k] = rest[g, k] + (g << 18)
             return 0
 
-        lax.fori_loop(0, totals[g * 4 + 3, 0], entry, 0)
-        count = count + totals[g * 4 + 3, 0]
+        lax.fori_loop(0, totals[g * 8 + 4, 0], entry, 0)
+        count = count + totals[g * 8 + 4, 0]
     for u in range(UNROLL - 1):
         flat[count + u] = TRASH
 
@@ -403,40 +409,73 @@
         n_down = send(src(3, 0, half), near.at[h, 1, pl.ds(0, half)], to(3))
         return o_up, o_down, n_up, n_down
 
-    def relay(copies, val, n, h, to, opp, near, fwd):
-        half = n // 2
+    def relay(copies, val, h, to):
+        late = []
         copies[0].wait_recv()
-        fwd[h, 0] = val(1, 0, half) + opp[h, 0]
-        f_up = send(fwd.at[h, 0], near.at[h, 0, pl.ds(0, half)], to(1))
+        for lo in (4, 0):
+            fwd[h, 0, pl.ds(lo, 4)] = val(1, lo, 4) + opp[h, 0, pl.ds(lo, 4)]
+            late.append(send(fwd.at[h, 0, pl.ds(lo, 4)], near.at[h, 0, pl.ds(lo, 4)], to(1)))
         copies[1].wait_recv()
-        fwd[h, 1] = val(3, half, half) + opp[h, 1]
-        f_down = send(fwd.at[h, 1], near.at[h, 1, pl.ds(half, half)], to(3))
-        return copies[2], copies[3], f_up, f_down
+        for lo in (0, 4):
+            fwd[h, 1, pl.ds(lo, 4)] = val(3, 8 + lo, 4) + opp[h, 1, pl.ds(lo, 4)]
+            late.append(send(fwd.at[h, 1, pl.ds(lo, 4)], near.at[h, 1, pl.ds(8 + lo, 4)], to(3)))
+        return [copies[2], copies[3]] + late
 
     ways = ((along_y, along_x), (along_x, along_y))
+
+    def value(h):
+        return lambda r, lo, size: part[pl.ds(h * 64 + r * 16 + lo, size)]
+
     firsts = []
     for h in range(2):
         firsts.append(
             begin(lambda r, lo, size: part.at[pl.ds(h * 64 + r * 16 + lo, size)], 16, h, ways[h][0], opp, near)
         )
+    for h in range(2):
+        firsts[h] = relay(firsts[h], value(h), h, ways[h][0])
+
+    def settle(h, r):
+        at = pl.ds(r * 4, 4)
+        mid[h, at] = part[pl.ds(h * 64 + r * 4, 4)] + (near[h, 0, at] + near[h, 1, at])
+
     seconds = []
     for h in range(2):
-        firsts[h] = relay(
-            firsts[h], lambda r, lo, size: part[pl.ds(h * 64 + r * 16 + lo, size)], 16, h, ways[h][0], opp, near, fwd
-        )
-    for h in range(2):
-        for copy in firsts[h]:
-            copy.wait_recv()
-        mid[h] = part[pl.ds(h * 64, 16)] + (near[h, 0] + near[h, 1])
-        seconds.append(
-            begin(lambda r, lo, size: mid.at[h, pl.ds(r * 4 + lo, size)], 4, h, ways[h][1], mid_opp, mid_near)
-        )
-    for h in range(2):
-        seconds[h] = relay(
-            seconds[h], lambda r, lo, size: mid[h, pl.ds(r * 4 + lo, size)], 4, h, ways[h][1], mid_opp, mid_near, mid_fwd
-        )
-    for h in range(2):
-        for copy in seconds[h]:
+        to = ways[h][1]
+        n_up, n_down, up_1, up_0, down_2, down_3 = firsts[h]
+        n_up.wait_recv()
+        n_down.wait_recv()
+        down_2.wait_recv()
+        settle(h, 2)
+        two = [
+            send(mid.at[h, pl.ds(8, 2)], mid_opp.at[h, 0], to(1)),
+            send(mid.at[h, pl.ds(10, 2)], mid_opp.at[h, 1], to(3)),
+        ]
+        up_1.wait_recv()
+        settle(h, 1)
+        two.append(send(mid.at[h, pl.ds(6, 2)], mid_near.at[h, 0, pl.ds(2, 2)], to(1)))
+        seconds.append(two)
+    for h in range(2):
+        to = ways[h][1]
+        n_up, n_down, up_1, up_0, down_2, down_3 = firsts[h]
+        down_3.wait_recv()
+        settle(h, 3)
+        seconds[h].append(send(mid.at[h, pl.ds(12, 2)], mid_near.at[h, 1, pl.ds(0, 2)], to(3)))
+    ends = []
+    for h in range(2):
+        to = ways[h][1]
+        o_up, o_down, n_up, n_down = seconds[h]
+        o_up.wait_recv()
+        mid_fwd[h, 0] = mid[h, pl.ds(4, 2)] + mid_opp[h, 0]
+        f_up = send(mid_fwd.at[h, 0], mid_near.at[h, 0, pl.ds(0, 2)], to(1))
+        o_down.wait_recv()
+        mid_fwd[h, 1] = mid[h, pl.ds(14, 2)] + mid_opp[h, 1]
+        f_down = send(mid_fwd.at[h, 1], mid_near.at[h, 1, pl.ds(2, 2)], to(3))
+        ends.append((n_up, n_down, f_up, f_down))
+    for h in range(2):
+        firsts[h][3].wait_recv()
+        settle(h, 0)
+    for h in range(2):
+        for copy in ends[h]:
             copy.wait_recv()
         out[pl.ds(h * 4, 4)] = mid[h, pl.ds(0, 4)] + (mid_near[h, 0] + mid_near[h, 1])
     for copy in sent:
@@ -457,10 +496,10 @@
         out_shape=(
             jax.ShapeDtypeStruct((2, EB, 2 * TR, KH), BF16),
             jax.ShapeDtypeStruct((EB, TR, KH), F32),
-            jax.ShapeDtypeStruct((2, FIXED[0] - REUSED + FIXED[1], TR, TR), F32),
+            jax.ShapeDtypeStruct((2, BEGIN[2] + FIXED[2], TR, TR), F32),
             jax.ShapeDtypeStruct((8, 128), jnp.int32),
             jax.ShapeDtypeStruct((8, REST), jnp.int32),
-            jax.ShapeDtypeStruct((8, 128), jnp.int32),
+            jax.ShapeDtypeStruct((16, 128), jnp.int32),
         ),
         in_specs=[hbm, hbm, smem, hbm],
         out_specs=(vmem,) * 6,
@@ -505,8 +544,8 @@
             pltpu.VMEM((2, 2, 2, TR, TR), F32),
             pltpu.VMEM((2, 2, 4, TR, TR), F32),
             pltpu.VMEM((2, 2, 2, TR, TR), F32),
-            dma((24,)),
-            dma((24,)),
+            dma((28,)),
+            dma((28,)),
         ],
         compiler_params=pltpu.CompilerParams(collective_id=1, has_side_effects=True, vmem_limit_bytes=14 * 2**20),
         name="scatter",

time: 141 us -> 138 us (0.979)
  Pallas kernels: 138 us -> 136 us
where the time goes in v5:
time: 138 us; the launch traced here: 137 us
  Pallas kernels  136 us (99%)
    pallas_call x1, Pallas kernels, per_device(): pl.pallas_call(gather_kernel, out_shape=(jax.ShapeDtypeStruct((2, EB, 2 *...  80 us
    pallas_call x1, Pallas kernels, per_device(): pl.pallas_call(scatter_kernel, out_shape=jax.ShapeDtypeStruct((8, TR, TR)...  47.5 us
    pallas_call x1, Pallas kernels, per_device(): pl.pallas_call(tiles_kernel, out_shape=jax.ShapeDtypeStruct((TRASH + 1, T...  8 us

profile of v5, /device:TPU:1, one launch (start us, length us, event | category | flops | bytes accessed | tf_op | source)
XLA Modules:
  0.0 137.1 jit_solution(917396644949380515)
XLA Ops:
  0.7 80.0 %gather.1 = (bf16[2,32,256,512]{3,2,1,0:T(8,128)(2,1)S(1)}, f32[32,128,512]{2,1,0:T(8,128)S(1)}, f32[2,60,128,128]{3,2,1,0:T(8,128)S(1)}, s32[8,128]{1,0:T(8,128...) custom-call(f32[512,1024]{1,0:T(8,128)} %bitcast.1, s32[16,32,32]{2,1,0:T(8,128)} %parents.1, s32[1]{0:T(128)S(6)} %copy.6.sizes, ...), custom_call_target="tpu_custom_call" | custom-call | tf_op jit(solution)/shard_map/gather/pallas_call | solution.py:494
  80.7 8.0 %tiles.1.part = f32[129,128,128]{2,1,0:T(8,128)S(1)} custom-call(s32[8,128]{1,0:T(8,128)S(1)} %get-tuple-element.11.codes, s32[8,256]{1,0:T(8,128)S(1)} %get-tuple-element.12.rest, s32[16,128]{1,0:T(8,128)S(1)} %get-tuple-element.13.totals, bf16[2,32,256,512]{3,2,1,0:T(8,128)(2,1)S(1)} %get-tuple-element.14.held, ...), custom_call_target="tpu_custom_call" | custom-call | tf_op jit(solution)/shard_map/tiles/pallas_call | solution.py:525
  88.7 0.0 copy-start
  88.7 47.5 %scatter.1 = f32[8,128,128]{2,1,0:T(8,128)S(1)} custom-call(f32[129,128,128]{2,1,0:T(8,128)S(1)} %tiles.1.part), custom_call_target="tpu_custom_call" | custom-call | tf_op jit(solution)/shard_map/scatter/pallas_call | solution.py:534
  136.3 0.0 copy-done
  136.3 0.9 sub.3
Async XLA Ops:
  88.7 47.5 %copy-start = (f32[8,128,128]{2,1,0:T(8,128)S(1)}, f32[8,128,128]{2,1,0:T(8,128)}, u32[]{:S(2)}) copy-start(f32[8,128,128]{2,1,0:T(8,128)} %param.9) | copy-start | bytes 1572868

commit v6 on v5

--- a/solution.py
+++ b/solution.py
@@ -12,17 +12,27 @@
 CB = 4
 EB = 32
 UNROLL = 8
-BATCH = 16
-FIXED = (48, 24, 28, 16)
-REUSED = 40
-FREED = (20, 21, 22, 23, 28, 29, 30, 31)
-BEGIN = (0, 8, 32)
+FIXED = (16, 32, 24, 28, 20)
+LEVELS = len(FIXED)
+STAGED = 64
 REST = 256
 TRASH = 128
 
 MESH = pl.DeviceIdType.MESH
 F32 = jnp.float32
 BF16 = jnp.bfloat16
+
+
+def homes(g):
+    return (
+        (0, 0, 16, True, g * 4),
+        (1, 0, 24, True, 8 + g * 6),
+        (1, 24, 8, False, 0),
+        (2, 0, 24, False, 8),
+        (3, 0, 28, False, 32),
+        (4, 0, 16, True, 20 + g * 8),
+        (4, 16, 4, False, 60),
+    )
 
 
 def position():
@@ -134,7 +144,8 @@
         return ((((block >> 4) ^ xh) << 4) + ((((block >> 2) - z) & 3) << 2)) + (block & 3)
 
     def level_of(s):
-        return jnp.where(s < 20, 0, jnp.where((s >= 24) & (s < 28), 3, 1) + (s & 1))
+        early = jnp.where((s < 8) | ((s >= 12) & (s < 16)), 0, 1)
+        return jnp.where(s < 20, early, jnp.where((s >= 24) & (s < 28), 4, 2) + (s & 1))
 
     a_slot, b_slot = place_of(row), place_of(col)
     level = jnp.maximum(level_of(a_slot), level_of(b_slot))
@@ -178,33 +189,34 @@
         first = place < 4
         at = jnp.where(first, ry * 4 + rx, 16 + rx * 4 + ry) * 4 + (place & 3)
         code = ((b_slot << 13) + (a_slot << 8) + at).astype(F32)
-        over = level == 4
-        for n in range(4):
-            where, many = places(hit & (level == n))
-            codes[g * 4 + n : g * 4 + n + 1, 0 : FIXED[n]] = listed(where, code, FIXED[n])
+        late = hit & (level == LEVELS)
+        over = hit & (level < 0)
+        for n in range(LEVELS):
+            where, many = places((hit & (level == n)) | over)
+            codes[g * 8 + n : g * 8 + n + 1, 0 : FIXED[n]] = listed(where, code, FIXED[n])
             totals[g * 8 + n : g * 8 + n + 1, :] = jnp.broadcast_to(many, (1, 128))
-            over = over | (where >= FIXED[n])
-        where, many = places(hit & over)
+            over = where >= FIXED[n]
+        where, many = places(late | over)
         rest[g : g + 1, :] = listed(where, code, REST)
-        totals[g * 8 + 4 : g * 8 + 5, :] = jnp.broadcast_to(many, (1, 128))
+        totals[g * 8 + LEVELS : g * 8 + LEVELS + 1, :] = jnp.broadcast_to(many, (1, 128))
 
     def product(g, n, t):
-        c = code_s[g * 4 + n, t]
+        c = code_s[g * 8 + n, t]
         d = lax.dot_general(
             split[g, (c >> 8) & 31], split[g, (c >> 13) & 31], (((1,), (1,)), ((), ())),
             preferred_element_type=F32,
         )
         return d[:TR, :TR] + (d[:TR, TR:] + d[TR:, :TR])
 
-    def products(g, n, begin, end):
-        for t in range(begin, end):
-            lanes = pl.ds((t % 4) * TR, TR)
-            if n == 3:
-                other[FREED[g * 4 + t // 4], :, lanes] = product(g, n, t)
-            elif n == 0 and t < REUSED:
-                other[g * 10 + t // 4, :, lanes] = product(g, n, t)
-            else:
-                staged[g, BEGIN[n] + t - (REUSED if n == 0 else 0)] = product(g, n, t)
+    def products(g, n):
+        for level_, first, many, again, base in homes(g):
+            if level_ == n:
+                for t in range(many):
+                    d = product(g, n, first + t)
+                    if again:
+                        other[base + t // 4, :, pl.ds((t % 4) * TR, TR)] = d
+                    else:
+                        staged[g, base + t] = d
 
     def convert(g, s):
         src = mine if g == 0 else other
@@ -237,6 +249,10 @@
         convert(1, t)
 
     plan(0)
+    def drain_all():
+        while twin_queue:
+            drain()
+
     fs_copy.wait_recv()
     for c, load in zip((0, 1, 2, 3), loads):
         load.wait()
@@ -251,6 +267,11 @@
         if d >= 2:
             send_z(mine.at[slot(0, 1, d)], 0, 2, d, down)
         take(slot(0, 1, d))
+        if i == 3:
+            code_copy.wait()
+            drain_all()
+            products(0, 0)
+            products(1, 0)
         e = (0, 2, 1, 3)[i]
         s = slot(1, 0, e)
         arrived(s)
@@ -259,21 +280,13 @@
         take(s)
         if i == 0:
             plan(1)
-        if i == 2:
+        if i == 1:
             code_copy = pltpu.make_async_copy(codes, code_s, local.at[8])
             code_copy.start()
     for e in (0, 2, 1, 3):
         arrived(slot(0, 2, e))
         take(slot(0, 2, e))
-    code_copy.wait()
-    while twin_queue:
-        drain()
-    work = [(0, 0), (1, 0), (0, 1), (1, 1), (0, 2), (1, 2)]
-
-    def batch():
-        g, first = work.pop(0)
-        products(g, 0, first * BATCH, (first + 1) * BATCH)
-
+    drain_all()
     for e in (0, 2, 1, 3):
         s = slot(1, 3, e)
         arrived(s)
@@ -285,32 +298,28 @@
         if e >= 2:
             send_z(mine.at[s], 1, 2, e, down)
         take(s)
-        if e in (0, 2):
-            batch()
-            batch()
+        if e == 0:
+            products(0, 1)
         if e == 2:
-            while twin_queue:
-                drain()
-            batch()
-            batch()
-        if e in (1, 3):
-            products(0 if e == 1 else 1, 1, 0, FIXED[1])
-    while twin_queue:
-        drain()
-    products(0, 2, 0, FIXED[2])
+            products(1, 1)
+            drain_all()
+        if e == 1:
+            products(0, 2)
+        if e == 3:
+            products(1, 2)
+    drain_all()
+    products(0, 3)
     for e in (0, 2):
         arrived(slot(1, 2, e))
         take(slot(1, 2, e))
-    products(1, 2, 0, FIXED[2])
-    while twin_queue:
-        drain()
-    products(0, 3, 0, FIXED[3])
-    products(1, 3, 0, FIXED[3])
+    products(1, 3)
+    drain_all()
+    products(0, 4)
+    products(1, 4)
     for e in (1, 3):
         arrived(slot(1, 2, e))
         take(slot(1, 2, e))
-    while twin_queue:
-        drain()
+    drain_all()
     for copy in sent:
         copy.wait_send()
 
@@ -321,37 +330,30 @@
         return 0
 
     lax.fori_loop(0, TRASH + 1, clear, 0)
-    def add(g, n, t, value):
-        at = jnp.where(t < totals[g * 8 + n, 0], codes[g * 4 + n, t] & 255, TRASH)
-        acc[at] += value
-
     for g in range(2):
-        def four(i, _):
-            for u in range(4):
-                add(g, 0, i * 4 + u, reused[g * 10 + i, :, pl.ds(u * TR, TR)])
-            return 0
-
-        lax.fori_loop(0, REUSED // 4, four, 0)
-        for t in range(REUSED, FIXED[0]):
-            add(g, 0, t, staged[g, t - REUSED])
-
-        for n in (1, 2):
+        for n, first, many, again, base in homes(g):
+            wide = 8 if many % 8 == 0 else 4
+            total = totals[g * 8 + n, 0]
+
             def some(i, _):
-                for u in range(4):
-                    add(g, n, i * 4 + u, staged[g, BEGIN[n] + i * 4 + u])
+                for u in range(wide):
+                    t = first + i * wide + u
+                    at = jnp.where(t < total, codes[g * 8 + n, t] & 255, TRASH)
+                    if again:
+                        acc[at] += reused[base + i * (wide // 4) + u // 4, :, pl.ds((u % 4) * TR, TR)]
+                    else:
+                        acc[at] += staged[g, base + i * wide + u]
                 return 0
 
-            lax.fori_loop(0, FIXED[n] // 4, some, 0)
-        for t in range(FIXED[3]):
-            add(g, 3, t, reused[FREED[g * 4 + t // 4], :, pl.ds((t % 4) * TR, TR)])
+            lax.fori_loop(0, many // wide, some, 0)
     count = 0
     for g in range(2):
         def entry(k, _):
             flat[count + k] = rest[g, k] + (g << 18)
             return 0
 
-        lax.fori_loop(0, totals[g * 8 + 4, 0], entry, 0)
-        count = count + totals[g * 8 + 4, 0]
+        lax.fori_loop(0, totals[g * 8 + LEVELS, 0], entry, 0)
+        count = count + totals[g * 8 + LEVELS, 0]
     for u in range(UNROLL - 1):
         flat[count + u] = TRASH
 
@@ -496,8 +498,8 @@
         out_shape=(
             jax.ShapeDtypeStruct((2, EB, 2 * TR, KH), BF16),
             jax.ShapeDtypeStruct((EB, TR, KH), F32),
-            jax.ShapeDtypeStruct((2, BEGIN[2] + FIXED[2], TR, TR), F32),
-            jax.ShapeDtypeStruct((8, 128), jnp.int32),
+            jax.ShapeDtypeStruct((2, STAGED, TR, TR), F32),
+            jax.ShapeDtypeStruct((16, 128), jnp.int32),
             jax.ShapeDtypeStruct((8, REST), jnp.int32),
             jax.ShapeDtypeStruct((16, 128), jnp.int32),
         ),
@@ -509,7 +511,7 @@
             pltpu.VMEM((8, KH), jnp.int32),
             pltpu.VMEM((2, EB, EB), jnp.int32),
             pltpu.SMEM((16,), jnp.int32),
-            pltpu.SMEM((8, 128), jnp.int32),
+            pltpu.SMEM((16, 128), jnp.int32),
             pltpu.VMEM((REST, 128), F32),
             dma((4,)),
             dma((24,)),

time: 138 us -> 138 us (level)
  no operation moved by 1% of the time
where the time goes in v6:
time: 138 us
  Pallas kernels  136 us (99%)
    pallas_call x1, Pallas kernels, per_device(): pl.pallas_call(gather_kernel, out_shape=(jax.ShapeDtypeStruct((2, EB, 2 *...  80.5 us
    pallas_call x1, Pallas kernels, per_device(): pl.pallas_call(scatter_kernel, out_shape=jax.ShapeDtypeStruct((8, TR, TR)...  48.5 us
    pallas_call x1, Pallas kernels, per_device(): pl.pallas_call(tiles_kernel, out_shape=jax.ShapeDtypeStruct((TRASH + 1, T...  7.15 us

profile of v6, /device:TPU:1, one launch (start us, length us, event | category | flops | bytes accessed | tf_op | source)
XLA Modules:
  0.0 137.6 jit_solution(617449312586710995)
XLA Ops:
  0.7 80.5 %gather.1 = (bf16[2,32,256,512]{3,2,1,0:T(8,128)(2,1)S(1)}, f32[32,128,512]{2,1,0:T(8,128)S(1)}, f32[2,64,128,128]{3,2,1,0:T(8,128)S(1)}, s32[16,128]{1,0:T(8,12...) custom-call(f32[512,1024]{1,0:T(8,128)} %bitcast.1, s32[16,32,32]{2,1,0:T(8,128)} %parents.1, s32[1]{0:T(128)S(6)} %copy.6.sizes, ...), custom_call_target="tpu_custom_call" | custom-call | tf_op jit(solution)/shard_map/gather/pallas_call | solution.py:496
  81.1 7.2 %tiles.1.part = f32[129,128,128]{2,1,0:T(8,128)S(1)} custom-call(s32[16,128]{1,0:T(8,128)S(1)} %get-tuple-element.11.codes, s32[8,256]{1,0:T(8,128)S(1)} %get-tuple-element.12.rest, s32[16,128]{1,0:T(8,128)S(1)} %get-tuple-element.13.totals, bf16[2,32,256,512]{3,2,1,0:T(8,128)(2,1)S(1)} %get-tuple-element.14.held, ...), custom_call_target="tpu_custom_call" | custom-call | tf_op jit(solution)/shard_map/tiles/pallas_call | solution.py:527
  88.3 0.0 copy-start
  88.3 48.5 %scatter.1 = f32[8,128,128]{2,1,0:T(8,128)S(1)} custom-call(f32[129,128,128]{2,1,0:T(8,128)S(1)} %tiles.1.part), custom_call_target="tpu_custom_call" | custom-call | tf_op jit(solution)/shard_map/scatter/pallas_call | solution.py:536
  136.8 0.0 copy-done
  136.8 0.9 sub.3
Async XLA Ops:
  88.3 48.5 %copy-start = (f32[8,128,128]{2,1,0:T(8,128)S(1)}, f32[8,128,128]{2,1,0:T(8,128)}, u32[]{:S(2)}) copy-start(f32[8,128,128]{2,1,0:T(8,128)} %param.9) | copy-start | bytes 1572868

commit v7 on v6

--- a/solution.py
+++ b/solution.py
@@ -12,6 +12,7 @@
 CB = 4
 EB = 32
 UNROLL = 8
+MERGED = 4
 FIXED = (16, 32, 24, 28, 20)
 LEVELS = len(FIXED)
 STAGED = 64
@@ -330,22 +331,6 @@
         return 0
 
     lax.fori_loop(0, TRASH + 1, clear, 0)
-    for g in range(2):
-        for n, first, many, again, base in homes(g):
-            wide = 8 if many % 8 == 0 else 4
-            total = totals[g * 8 + n, 0]
-
-            def some(i, _):
-                for u in range(wide):
-                    t = first + i * wide + u
-                    at = jnp.where(t < total, codes[g * 8 + n, t] & 255, TRASH)
-                    if again:
-                        acc[at] += reused[base + i * (wide // 4) + u // 4, :, pl.ds((u % 4) * TR, TR)]
-                    else:
-                        acc[at] += staged[g, base + i * wide + u]
-                return 0
-
-            lax.fori_loop(0, many // wide, some, 0)
     count = 0
     for g in range(2):
         def entry(k, _):
@@ -354,20 +339,62 @@
 
         lax.fori_loop(0, totals[g * 8 + LEVELS, 0], entry, 0)
         count = count + totals[g * 8 + LEVELS, 0]
-    for u in range(UNROLL - 1):
-        flat[count + u] = TRASH
+
+    def blank(k, _):
+        flat[k] = TRASH
+        return 0
+
+    lax.fori_loop(count, jnp.maximum(count + UNROLL, MERGED * UNROLL), blank, 0)
+
+    def add(g, n, t, value):
+        at = jnp.where(t < totals[g * 8 + n, 0], codes[g * 8 + n, t] & 255, TRASH)
+        acc[at] += value
+
+    def fixed(g, n, first, again, base, per, i, u):
+        t = first + i * per + u
+        if again:
+            add(g, n, t, reused[base + i * (per // 4) + u // 4, :, pl.ds((u % 4) * TR, TR)])
+        else:
+            add(g, n, t, staged[g, base + i * per + u])
+
+    def rest_tile(t):
+        c = flat[t]
+        g, b, a, at = c >> 18, (c >> 13) & 31, (c >> 8) & 31, c & 255
+        d = lax.dot_general(
+            held[g, a], held[g, b], (((1,), (1,)), ((), ())), preferred_element_type=F32
+        )
+        return at, d
+
+    def put(at, d):
+        acc[at] += d[:TR, :TR] + (d[:TR, TR:] + d[TR:, :TR])
+
+    runs, odd = [], []
+    for g in range(2):
+        for n, first, many, again, base in homes(g):
+            grain = 4 * MERGED if again else MERGED
+            even = many // grain * grain
+            runs += [(g, n, first, again, base, even // MERGED, u) for u in range(even // MERGED)]
+            odd += [(g, n, first + t, again, base + (t // 4 if again else t), t % 4 if again else 0) for t in range(even, many)]
+
+    def merged(i, _):
+        share = -(-len(runs) // UNROLL)
+        for k in range(UNROLL):
+            at, d = rest_tile(i * UNROLL + k)
+            for g, n, first, again, base, per, u in runs[k * share : (k + 1) * share]:
+                fixed(g, n, first, again, base, per, i, u)
+            put(at, d)
+        return 0
+
+    lax.fori_loop(0, MERGED, merged, 0)
+    for g, n, t, again, place, lane in odd:
+        add(g, n, t, reused[place, :, pl.ds(lane * TR, TR)] if again else staged[g, place])
 
     def several(i, _):
-        for u in range(UNROLL):
-            c = flat[i * UNROLL + u]
-            g, b, a, at = c >> 18, (c >> 13) & 31, (c >> 8) & 31, c & 255
-            d = lax.dot_general(
-                held[g, a], held[g, b], (((1,), (1,)), ((), ())), preferred_element_type=F32
-            )
-            acc[at] += d[:TR, :TR] + (d[:TR, TR:] + d[TR:, :TR])
+        for k in range(UNROLL):
+            put(*rest_tile(i * UNROLL + k))
         return 0
 
-    lax.fori_loop(0, (count + UNROLL - 1) // UNROLL, several, 0)
+    lax.fori_loop(MERGED, (count + UNROLL - 1) // UNROLL, several, 0)
 
 
 def scatter_kernel(
@@ -529,7 +556,7 @@
         out_shape=jax.ShapeDtypeStruct((TRASH + 1, TR, TR), F32),
         in_specs=[smem, smem, smem, vmem, vmem, vmem],
         out_specs=vmem,
-        scratch_shapes=[pltpu.SMEM((2 * REST + UNROLL,), jnp.int32)],
+        scratch_shapes=[pltpu.SMEM((2 * REST + MERGED * UNROLL,), jnp.int32)],
         compiler_params=pltpu.CompilerParams(vmem_limit_bytes=4 * 2**20),
         name="tiles",
     )(codes, rest, totals, split, reused, staged)

time: 138 us -> 136 us (0.986)
  Pallas kernels: 136 us -> 133 us
    pallas_call x1, Pallas kernels: 48.5 us -> 46.6 us  [per_device(): pl.pallas_call(scatter_kernel, out_shape=jax.ShapeDtypeStruct((8, TR, TR)...]
where the time goes in v7:
time: 136 us; the launch traced here: 134 us
  Pallas kernels  133 us (98%)
    pallas_call x1, Pallas kernels, per_device(): pl.pallas_call(gather_kernel, out_shape=(jax.ShapeDtypeStruct((2, EB, 2 *...  80.5 us
    pallas_call x1, Pallas kernels, per_device(): pl.pallas_call(scatter_kernel, out_shape=jax.ShapeDtypeStruct((8, TR, TR)...  46.6 us
    pallas_call x1, Pallas kernels, per_device(): pl.pallas_call(tiles_kernel, out_shape=jax.ShapeDtypeStruct((TRASH + 1, T...  5.87 us

profile of v7, /device:TPU:1, one launch (start us, length us, event | category | flops | bytes accessed | tf_op | source)
XLA Modules:
  0.0 134.5 jit_solution(15415470890117396058)
XLA Ops:
  0.7 80.5 %gather.1 = (bf16[2,32,256,512]{3,2,1,0:T(8,128)(2,1)S(1)}, f32[32,128,512]{2,1,0:T(8,128)S(1)}, f32[2,64,128,128]{3,2,1,0:T(8,128)S(1)}, s32[16,128]{1,0:T(8,12...) custom-call(f32[512,1024]{1,0:T(8,128)} %bitcast.1, s32[16,32,32]{2,1,0:T(8,128)} %parents.1, s32[1]{0:T(128)S(6)} %copy.6.sizes, ...), custom_call_target="tpu_custom_call" | custom-call | tf_op jit(solution)/shard_map/gather/pallas_call | solution.py:523
  81.1 5.9 %tiles.1.part = f32[129,128,128]{2,1,0:T(8,128)S(1)} custom-call(s32[16,128]{1,0:T(8,128)S(1)} %get-tuple-element.11.codes, s32[8,256]{1,0:T(8,128)S(1)} %get-tuple-element.12.rest, s32[16,128]{1,0:T(8,128)S(1)} %get-tuple-element.13.totals, bf16[2,32,256,512]{3,2,1,0:T(8,128)(2,1)S(1)} %get-tuple-element.14.held, ...), custom_call_target="tpu_custom_call" | custom-call | tf_op jit(solution)/shard_map/tiles/pallas_call | solution.py:554
  87.0 0.0 copy-start
  87.0 46.6 %scatter.1 = f32[8,128,128]{2,1,0:T(8,128)S(1)} custom-call(f32[129,128,128]{2,1,0:T(8,128)S(1)} %tiles.1.part), custom_call_target="tpu_custom_call" | custom-call | tf_op jit(solution)/shard_map/scatter/pallas_call | solution.py:563
  133.6 0.0 copy-done
  133.6 0.9 sub.3
Async XLA Ops:
  87.0 46.6 %copy-start = (f32[8,128,128]{2,1,0:T(8,128)S(1)}, f32[8,128,128]{2,1,0:T(8,128)}, u32[]{:S(2)}) copy-start(f32[8,128,128]{2,1,0:T(8,128)} %param.9) | copy-start | bytes 1572868

commit v8 on v7

--- a/solution.py
+++ b/solution.py
@@ -121,9 +121,6 @@
 
     fs[...] = jnp.full((8, KH), sizes[0], jnp.int32)
     loads = []
-    for c in (0, 2, 1, 3):
-        s = slot(1, 0, c)
-        send(x.at[rows(c), across_cols], mine.at[s], x_send.at[c], recv.at[s], across)
     for c, d in ((0, 2), (1, 3), (2, 0), (3, 1)):
         send_z(x.at[rows(c), own_cols], 0, 3, c, up)
         send_z(x.at[rows(d), own_cols], 0, 1, d, down)
@@ -131,6 +128,9 @@
         load.start()
         loads.append(load)
 
+    for c in (0, 2, 1, 3):
+        s = slot(1, 0, c)
+        send(x.at[rows(c), across_cols], mine.at[s], x_send.at[c], recv.at[s], across)
     for copy in small:
         copy.wait()
     send(fs, fs_other, fs_sem.at[0], fs_sem.at[1], twin)
@@ -316,10 +316,10 @@
     products(1, 3)
     drain_all()
     products(0, 4)
-    products(1, 4)
     for e in (1, 3):
         arrived(slot(1, 2, e))
         take(slot(1, 2, e))
+    products(1, 4)
     drain_all()
     for copy in sent:
         copy.wait_send()

time: 136 us -> 135 us (level)
  no operation moved by 1% of the time
where the time goes in v8:
time: 135 us
  Pallas kernels  133 us (99%)
    pallas_call x1, Pallas kernels, per_device(): pl.pallas_call(gather_kernel, out_shape=(jax.ShapeDtypeStruct((2, EB, 2 *...  79.5 us
    pallas_call x1, Pallas kernels, per_device(): pl.pallas_call(scatter_kernel, out_shape=jax.ShapeDtypeStruct((8, TR, TR)...  47.1 us
    pallas_call x1, Pallas kernels, per_device(): pl.pallas_call(tiles_kernel, out_shape=jax.ShapeDtypeStruct((TRASH + 1, T...  6.65 us

profile of v8, /device:TPU:1, one launch (start us, length us, event | category | flops | bytes accessed | tf_op | source)
XLA Modules:
  0.0 134.8 jit_solution(3308444932783470061)
XLA Ops:
  0.7 79.5 %gather.1 = (bf16[2,32,256,512]{3,2,1,0:T(8,128)(2,1)S(1)}, f32[32,128,512]{2,1,0:T(8,128)S(1)}, f32[2,64,128,128]{3,2,1,0:T(8,128)S(1)}, s32[16,128]{1,0:T(8,12...) custom-call(f32[512,1024]{1,0:T(8,128)} %bitcast.1, s32[16,32,32]{2,1,0:T(8,128)} %parents.1, s32[1]{0:T(128)S(6)} %copy.6.sizes, ...), custom_call_target="tpu_custom_call" | custom-call | tf_op jit(solution)/shard_map/gather/pallas_call | solution.py:523
  80.2 6.7 %tiles.1.part = f32[129,128,128]{2,1,0:T(8,128)S(1)} custom-call(s32[16,128]{1,0:T(8,128)S(1)} %get-tuple-element.11.codes, s32[8,256]{1,0:T(8,128)S(1)} %get-tuple-element.12.rest, s32[16,128]{1,0:T(8,128)S(1)} %get-tuple-element.13.totals, bf16[2,32,256,512]{3,2,1,0:T(8,128)(2,1)S(1)} %get-tuple-element.14.held, ...), custom_call_target="tpu_custom_call" | custom-call | tf_op jit(solution)/shard_map/tiles/pallas_call | solution.py:554
  86.8 0.0 copy-start
  86.8 47.1 %scatter.1 = f32[8,128,128]{2,1,0:T(8,128)S(1)} custom-call(f32[129,128,128]{2,1,0:T(8,128)S(1)} %tiles.1.part), custom_call_target="tpu_custom_call" | custom-call | tf_op jit(solution)/shard_map/scatter/pallas_call | solution.py:563
  133.9 0.0 copy-done
  133.9 0.9 sub.3
Async XLA Ops:
  86.8 47.1 %copy-start = (f32[8,128,128]{2,1,0:T(8,128)S(1)}, f32[8,128,128]{2,1,0:T(8,128)}, u32[]{:S(2)}) copy-start(f32[8,128,128]{2,1,0:T(8,128)} %param.9) | copy-start | bytes 1572868

commit v9 on v8

--- a/solution.py
+++ b/solution.py
@@ -398,7 +398,7 @@
 
 
 def scatter_kernel(
-    part, out, opp, near, fwd, mid, mid_opp, mid_near, mid_fwd,
+    part, entries, out, opp, near, fwd, mid, mid_opp, mid_near, mid_fwd,
     send_sem, recv_sem,
 ):
     p = position()
@@ -506,7 +506,7 @@
     for h in range(2):
         for copy in ends[h]:
             copy.wait_recv()
-        out[pl.ds(h * 4, 4)] = mid[h, pl.ds(0, 4)] + (mid_near[h, 0] + mid_near[h, 1])
+        out[pl.ds(h * 4, 4)] = entries[pl.ds(h * 4, 4)] - (mid[h, pl.ds(0, 4)] + (mid_near[h, 0] + mid_near[h, 1]))
     for copy in sent:
         copy.wait_send()
 
@@ -560,10 +560,10 @@
         compiler_params=pltpu.CompilerParams(vmem_limit_bytes=4 * 2**20),
         name="tiles",
     )(codes, rest, totals, split, reused, staged)
-    summed = pl.pallas_call(
+    return pl.pallas_call(
         scatter_kernel,
         out_shape=jax.ShapeDtypeStruct((8, TR, TR), F32),
-        in_specs=[vmem],
+        in_specs=[vmem, vmem],
         out_specs=vmem,
         scratch_shapes=[
             pltpu.VMEM((2, 2, 8, TR, TR), F32),
@@ -578,8 +578,7 @@
         ],
         compiler_params=pltpu.CompilerParams(collective_id=1, has_side_effects=True, vmem_limit_bytes=14 * 2**20),
         name="scatter",
-    )(part)
-    return parent_entries - summed
+    )(part, parent_entries)
 
 
 def solution(mesh):

time: 135 us -> 135 us (level)
  no operation moved by 1% of the time
where the time goes in v9:
time: 135 us; the launch traced here: 134 us
  Pallas kernels  132 us (98%)
    pallas_call x1, Pallas kernels, per_device(): pl.pallas_call(gather_kernel, out_shape=(jax.ShapeDtypeStruct((2, EB, 2 *...  79.5 us
    pallas_call x1, Pallas kernels, per_device(): pl.pallas_call(scatter_kernel, out_shape=jax.ShapeDtypeStruct((8, TR, TR)...  47 us
    pallas_call x1, Pallas kernels, per_device(): pl.pallas_call(tiles_kernel, out_shape=jax.ShapeDtypeStruct((TRASH + 1, T...  5.85 us

profile of v9, /device:TPU:1, one launch (start us, length us, event | category | flops | bytes accessed | tf_op | source)
XLA Modules:
  0.0 133.9 jit_solution(16968809408799306289)
XLA Ops:
  0.7 79.5 %gather.1 = (bf16[2,32,256,512]{3,2,1,0:T(8,128)(2,1)S(1)}, f32[32,128,512]{2,1,0:T(8,128)S(1)}, f32[2,64,128,128]{3,2,1,0:T(8,128)S(1)}, s32[16,128]{1,0:T(8,12...) custom-call(f32[512,1024]{1,0:T(8,128)} %bitcast.1, s32[16,32,32]{2,1,0:T(8,128)} %parents.1, s32[1]{0:T(128)S(6)} %copy.7.sizes, ...), custom_call_target="tpu_custom_call" | custom-call | tf_op jit(solution)/shard_map/gather/pallas_call | solution.py:523
  80.2 0.0 copy-start
  80.2 5.9 %tiles.1.part = f32[129,128,128]{2,1,0:T(8,128)S(1)} custom-call(s32[16,128]{1,0:T(8,128)S(1)} %get-tuple-element.11.codes, s32[8,256]{1,0:T(8,128)S(1)} %get-tuple-element.12.rest, s32[16,128]{1,0:T(8,128)S(1)} %get-tuple-element.13.totals, bf16[2,32,256,512]{3,2,1,0:T(8,128)(2,1)S(1)} %get-tuple-element.14.held, ...), custom_call_target="tpu_custom_call" | custom-call | tf_op jit(solution)/shard_map/tiles/pallas_call | solution.py:554
  86.0 0.0 copy-done
  86.0 47.0 %scatter.1 = f32[8,128,128]{2,1,0:T(8,128)S(1)} custom-call(f32[129,128,128]{2,1,0:T(8,128)S(1)} %tiles.1.part, f32[8,128,128]{2,1,0:T(8,128)S(1)} %copy-done), custom_call_target="tpu_custom_call" | custom-call | tf_op jit(solution)/shard_map/scatter/pallas_call | solution.py:563
  133.1 0.8 copy.8
Async XLA Ops:
  80.2 5.9 %copy-start = (f32[8,128,128]{2,1,0:T(8,128)S(1)}, f32[8,128,128]{2,1,0:T(8,128)}, u32[]{:S(2)}) copy-start(f32[8,128,128]{2,1,0:T(8,128)} %entries.1) | copy-start | bytes 1572868
